TPU v7x, 256 devices: a whole 4x4x8 slice. The times are simulated.
256 devices in a mesh: row: 16 (over y, z_lo, core), col: 16 (over z_hi, x).
Axes of the slice: x: 4, y: 4, z: 8 (z_hi: 4, z_lo: 2; z = z_hi * 2 + z_lo), core: 2. Of those that a mesh axis runs over, the one named last changes fastest.
Arguments:
- affinity: float32 [16384, 16384], P('row', 'col'), may hold values from 0.1 to 2600, as said below
- keep_words: int32 [16384, 5], P('row'), may hold values from 0 to 1073741823, as said below
Outputs:
- normalized: float32 [16384, 16384], P('row', 'col')
- degree: float32 [16384], P('row')
Inputs may be any that keep to these rules, and one draw needn't show every extreme that they name: `affinity`: all entries are positive. `keep_words`: bit b of word w in row i is 1 where the block of 128 columns numbered 30 * w + b is kept for row i. The block that holds column i is always kept in row i. Bits for block numbers of 128 or more carry no meaning.
All inputs are finite; a program needn't handle non-finite values.
Results may differ from a plain program's by a relative error of at most 0.0003.
Values sent between devices are 32-bit elements; how exact they have to be, the bound alone decides.
A program may use at most 64 MiB of HBM per device.

v0:
```python
import jax
import jax.numpy as jnp
from jax import lax
from jax.sharding import PartitionSpec as P

TILE = 128


def copy_for_each(x, axis):
    copies = jnp.broadcast_to(x, (lax.axis_size(axis), *x.shape))
    return lax.all_to_all(copies, axis, split_axis=0, concat_axis=0, tiled=True)


def over_copies(x, axis):
    return copy_for_each(x, axis).sum(axis=0)


def unpack_tiles(keep_words, first_tile, tile_count):
    shifts = jnp.arange(30, dtype=jnp.int32)
    bit_table = jnp.right_shift(keep_words[:, :, None], shifts[None, None, :]) & 1
    bit_table = bit_table.reshape(keep_words.shape[0], keep_words.shape[1] * 30)
    chosen = lax.dynamic_slice_in_dim(bit_table, first_tile, tile_count, 1)
    return jnp.repeat(chosen.astype(jnp.float32), TILE, axis=1)


def mirror_rows_first(pruned, row_count, col_count):
    block_rows, block_cols = pruned.shape
    fold_ratio = col_count // row_count
    strip_size = block_cols // row_count
    pieces = pruned.reshape(fold_ratio, block_cols, strip_size, row_count).transpose(2, 3, 0, 1)
    arrived = lax.all_to_all(
        lax.all_to_all(pieces, "row", split_axis=1, concat_axis=2, tiled=True),
        "col",
        split_axis=2,
        concat_axis=2,
        tiled=True,
    )
    arrived = lax.all_to_all(arrived, "row", split_axis=2, concat_axis=2, tiled=True)
    arrived = arrived.reshape(strip_size, row_count, fold_ratio, block_cols).transpose(2, 0, 1, 3)
    return arrived.reshape(block_rows, block_cols)


def on_device(affinity, keep_words):
    block_rows, block_cols = affinity.shape
    row_count = lax.axis_size("row")
    col_count = lax.axis_size("col")
    col_place = lax.axis_index("col")
    total_segments = block_rows * row_count
    kept_mask = unpack_tiles(keep_words, col_place * (block_cols // TILE), block_cols // TILE)
    pruned = affinity * kept_mask
    mirrored = mirror_rows_first(pruned, row_count, col_count)
    symmetric = 0.5 * (pruned + mirrored)
    degree_rows = over_copies(jnp.sum(symmetric, axis=1), "col")
    degree_cols = over_copies(jnp.sum(symmetric, axis=0), "row")
    left_scale = lax.rsqrt(degree_rows)
    right_scale = lax.rsqrt(degree_cols)
    normalized = total_segments * symmetric * left_scale[:, None] * right_scale[None, :]
    return (normalized, degree_rows / total_segments)


def solution(mesh):
    in_specs = (P("row", "col"), P("row", None))
    out_specs = (P("row", "col"), P("row"))
    return jax.shard_map(
        on_device, mesh=mesh, in_specs=in_specs, out_specs=out_specs, check_vma=False
    )
```

profile of v0, /device:TPU:1, one launch (start us, length us, event | category | flops | bytes accessed | tf_op | source)
XLA Modules:
  0.0 279.3 jit_solution(12702275744501847648)
XLA Ops:
  0.6 0.1 shift_right_arithmetic.23
  0.7 0.8 shift_right_arithmetic.20
  1.5 0.1 shift_right_arithmetic.21
  1.6 5.3 %copy.26 = f32[1024,1024]{0,1:T(8,128)} copy(f32[1024,1024]{1,0:T(8,128)} %param.2) | data formatting | bytes 8388608 | tf_op args[0]
  7.0 0.1 dynamic-slice
  7.0 0.1 fusion.1
  7.1 2.6 bitcast_multiply_fusion
  9.8 0.0 copy-start
  9.8 2.4 copy.27
  12.2 56.1 %all_to_all.34 = f32[64,16,1,1024]{3,0,2,1:T(8,128)S(1)} all-to-all(f32[64,16,1,1024]{3,0,2,1:T(8,128)S(1)} %copy.27), channel_id=1, replica_groups=mesh['row'=16,'col'=16] {'row'}, dimensions={1} | all-to-all | bytes 8388608 | tf_op jit(solution)/shard_map/all_to_all | solution.py:32
  68.3 82.2 %all_to_all.35 = f32[64,1,16,1024]{3,0,1,2:T(8,128)S(1)} all-to-all(f32[64,1,16,1024]{3,0,1,2:T(8,128)S(1)} %bitcast.12), channel_id=1, replica_groups=mesh['row'=16,'col'=16] {'col'}, dimensions={2} | all-to-all | bytes 8388608 | tf_op jit(solution)/shard_map/all_to_all | solution.py:31
  150.6 77.2 %all_to_all.36 = f32[64,1,16,1024]{3,0,1,2:T(8,128)S(1)} all-to-all(f32[64,1,16,1024]{3,0,1,2:T(8,128)S(1)} %all_to_all.35), channel_id=1, replica_groups=mesh['row'=16,'col'=16] {'row'}, dimensions={2} | all-to-all | bytes 8388608 | tf_op jit(solution)/shard_map/all_to_all | solution.py:38
  227.8 4.4 %copy.29 = f32[64,1,16,1024]{3,2,0,1:T(8,128)} copy(f32[64,1,16,1024]{3,0,1,2:T(8,128)S(1)} %all_to_all.36) | data formatting | bytes 8388608 | tf_op jit(solution)/shard_map/all_to_all | solution.py:38
  232.1 5.3 %copy.30 = f32[1024,1024]{0,1:T(8,128)} copy(f32[1024,1024]{1,0:T(8,128)} %bitcast.13) | data formatting | bytes 8388608 | tf_op jit(solution)/shard_map/reshape;transpose;reshape | solution.py:40
  237.5 6.4 %multiply_reduce_fusion.1 = (f32[1024]{0:T(1024)S(1)}, f32[1024]{0:T(1024)S(1)}, f32[1024,1024]{0,1:T(8,128)}) fusion(f32[1024,1024]{0,1:T(8,128)} %copy-done, f32[1024,1024]{0,1:T(8,128)} %copy.30), kind=kLoop, calls=%fused_computation.3 | loop fusion | flops 4192256 | bytes 12591104 | tf_op jit(solution)/shard_map/reduce_sum | solution.py:53
  243.9 13.1 %all_to_all.37 = f32[16,1,1024]{2,1,0:T(1,128)S(1)} all-to-all(f32[16,1,1024]{2,1,0:T(1,128)S(1)} %broadcast_in_dim.14), channel_id=1, replica_groups=mesh['row'=16,'col'=16] {'col'}, dimensions={0} | all-to-all | bytes 131072 | tf_op jit(solution)/shard_map/all_to_all | solution.py:11
  257.0 0.7 broadcast_in_dim.15
  257.6 5.9 %all-to-all-start.4 = ((f32[16,1,1024]{2,1,0:T(1,128)}), f32[16,1,1024]{2,1,0:T(1,128)S(1)}, u32[]{:S(2)}, u32[]{:S(2)}) async-start(f32[16,1,1024]{2,1,0:T(1,128)} %broadcast_in_dim.15), calls=%async_computation.4 | async-start | bytes 131072 | tf_op jit(solution)/shard_map/all_to_all | solution.py:11
  263.5 0.1 reduce_sum.37
  263.6 0.6 broadcast_multiply_fusion
  264.2 5.2 %all-to-all-done.4 = f32[16,1,1024]{2,1,0:T(1,128)S(1)} async-done(((f32[16,1,1024]{2,1,0:T(1,128)}), f32[16,1,1024]{2,1,0:T(1,128)S(1)}, u32[]{:S(2)}, u32[]{:S(2)}) %all-to-all-start.4) | async-done | bytes 65568 | tf_op jit(solution)/shard_map/all_to_all | solution.py:11
  269.4 0.1 reduce_sum.39
  269.5 4.5 %multiply_multiply_fusion = f32[1024,1024]{0,1:T(8,128)} fusion(f32[1024,1024]{0,1:T(8,128)} %get-tuple-element.14, f32[1024]{0:T(1024)S(1)} %rsqrt.15, f32[1024]{0:T(1024)S(1)} %get-tuple-element.16), kind=kLoop, calls=%fused_computation.1 | loop fusion | flops 2097152 | bytes 8396800 | tf_op jit(solution)/shard_map/mul | solution.py:57
  274.0 5.3 %copy.33 = f32[1024,1024]{1,0:T(8,128)} copy(f32[1024,1024]{0,1:T(8,128)} %multiply_multiply_fusion) | data formatting | bytes 8388608
  (4 shorter events, 0.0 us)
Async XLA Ops:
  9.8 2.5 copy-start
  257.6 11.8 %all-to-all-start.4 = ((f32[16,1,1024]{2,1,0:T(1,128)}), f32[16,1,1024]{2,1,0:T(1,128)S(1)}, u32[]{:S(2)}, u32[]{:S(2)}) async-start(f32[16,1,1024]{2,1,0:T(1,128)} %broadcast_in_dim.15), calls=%async_computation.4 | async-start | bytes 131072 | tf_op jit(solution)/shard_map/all_to_all | solution.py:11
where the time goes:
time: 280 us; the launch traced here: 279 us
  blocking collectives  229 us (82%)
  local copies, waits for them, and re-layouts  24.6 us (9%)
  other arithmetic  14.3 us (5%)
  starting transfers between devices  5.9 us (2%)
  waiting for transfers between devices  5.23 us (2%)
    all_to_all x1, blocking collectives, mirror_rows_first(): lax.all_to_all(lax.all_to_all(pieces, 'row', split_axis=1, concat_axis=2,...  82.2 us
    all_to_all x1, blocking collectives, mirror_rows_first(): lax.all_to_all(arrived, 'row', split_axis=2, concat_axis=2, tiled=True)  77.2 us
    all_to_all x1, blocking collectives, mirror_rows_first(): lax.all_to_all(pieces, 'row', split_axis=1, concat_axis=2, tiled=True)  56.1 us
    all_to_all x1, blocking collectives, copy_for_each(): return lax.all_to_all(copies, axis, split_axis=0, concat_axis=0, tiled=True)  13.1 us
    unnamed x4, local copies, waits for them, and re-layouts  10.7 us
    reduce_sum x1, other arithmetic, on_device(): degree_rows = over_copies(jnp.sum(symmetric, axis=1), 'col')  6.36 us
    all_to_all x1, starting transfers between devices, copy_for_each(): return lax.all_to_all(copies, axis, split_axis=0, concat_axis=0, tiled=True)  5.9 us
  transfers between devices with their start and end apart: 1, of which 1 were waited for; matrix products, arithmetic and copies ran while one was open for 0% of the time, Pallas kernels for 0%

commit v1 on v0

v1 whole, which is shorter than its diff:
```python
import functools

import jax
import jax.numpy as jnp
from jax import lax
from jax.experimental import pallas as pl
from jax.experimental.pallas import tpu as pltpu
from jax.sharding import PartitionSpec as P

TILE = 128
SIDE = 16
CHUNKS = 32
LOGICAL = pl.DeviceIdType.LOGICAL
OFFSETS = (
    (0, 0), (1, 0), (0, 1), (3, 0), (0, 3), (1, 1), (3, 3), (1, 3),
    (3, 1), (2, 0), (0, 2), (2, 1), (1, 2), (2, 3), (3, 2), (2, 2),
)


def packed(values):
    word = sum(v << (2 * n) for n, v in enumerate(values))
    return word - (1 << 32) if word >= 1 << 31 else word


X_STEPS = packed([o[0] for o in OFFSETS])
Y_STEPS = packed([o[1] for o in OFFSETS])


def kernel(aff, words, s_out, deg_out, block, mid, arrived, far_words, mask_rows, far_mask,
           col_sums, far_sums, row_sums, shares, half, half_far,
           load_sem, word_sem, leg_send, leg_recv, hop_send, final_sem,
           sum_sem, share_send, share_recv, half_sem, out_sem):
    row = lax.axis_index("row")
    col = lax.axis_index("col")
    me = row * SIDE + col
    partner = col * SIDE + row
    y, low, core = row // 4, (row // 2) % 2, row % 2
    high, x = col // 4, col % 4
    on_diagonal = row == col
    size = block.shape[0]
    chunk = size // CHUNKS
    groups = size // TILE

    def rows(n):
        return pl.ds(pl.multiple_of(n * chunk, chunk), chunk)

    def group(n):
        return pl.ds(pl.multiple_of(n * TILE, TILE), TILE)

    def place(cx, cy):
        return (cy * 4 + low * 2 + core) * SIDE + high * 4 + cx

    def steps(n):
        shift = 2 * (n % 16)
        return (X_STEPS >> shift) & 3, (Y_STEPS >> shift) & 3

    def mirror(device):
        return (device % SIDE) * SIDE + device // SIDE

    def to_partner(src, dst, sems):
        @pl.when(on_diagonal)
        def _():
            pltpu.make_async_copy(src, dst, sems.at[1]).start()

        @pl.when(jnp.logical_not(on_diagonal))
        def _():
            pltpu.make_async_remote_copy(
                src, dst, sems.at[0], sems.at[1], device_id=partner, device_id_type=LOGICAL
            ).start()

    def wait(ref, sem):
        pltpu.make_async_copy(ref, ref, sem).wait()

    def load(n):
        return pltpu.make_async_copy(aff.at[group(n)], block.at[group(n)], load_sem.at[n])

    to_partner(words, far_words, word_sem)

    def leg(n, carry):
        dx, dy = steps(n)
        relay = place((x + dx) % 4, (y + dy) % 4)
        direct = (n % 16 == 0) | (relay == partner)

        @pl.when(direct)
        def _():
            pltpu.make_async_remote_copy(
                aff.at[rows(n)], arrived.at[rows(n)], leg_send.at[n], final_sem.at[n // 4],
                device_id=partner, device_id_type=LOGICAL,
            ).start()

        @pl.when(jnp.logical_not(direct))
        def _():
            pltpu.make_async_remote_copy(
                aff.at[rows(n)], mid.at[rows(n)], leg_send.at[n], leg_recv.at[n],
                device_id=relay, device_id_type=LOGICAL,
            ).start()

        return carry

    def legs(first, last):
        @pl.when(jnp.logical_not(on_diagonal))
        def _():
            lax.fori_loop(first, last, leg, 0)

    def hop_of(n):
        dx, dy = steps(n)
        source = place((x + 4 - dx) % 4, (y + 4 - dy) % 4)
        target = mirror(source)
        return target, (n % 16 != 0) & (source != target) & (target != me)

    def hop(n, carry):
        target, used = hop_of(n)

        @pl.when(used)
        def _():
            wait(mid.at[rows(n)], leg_recv.at[n])
            pltpu.make_async_remote_copy(
                mid.at[rows(n)], arrived.at[rows(n)], hop_send.at[n], final_sem.at[n // 4],
                device_id=target, device_id_type=LOGICAL,
            ).start()

        return carry

    legs(0, CHUNKS // 2)

    def start_load(n, carry):
        load(n).start()
        return carry

    lax.fori_loop(0, groups, start_load, 0)

    @pl.when(on_diagonal)
    def _():
        def own(n, carry):
            pltpu.make_async_copy(aff.at[group(n)], arrived.at[group(n)], final_sem.at[n]).start()
            return carry

        lax.fori_loop(0, groups, own, 0)

    for t in range(groups):
        tile = col * groups + t
        bits = (words[pl.ds(tile // 30, 1), :] >> (tile % 30)) & 1
        mask_rows[t : t + 1, :] = bits.astype(jnp.float32)
    col_sums[...] = jnp.zeros_like(col_sums)

    def prune(n, carry):
        load(n).wait()
        mask = mask_rows[:, group(n)].T
        total = jnp.zeros((TILE, TILE), jnp.float32)
        for t in range(groups):
            lanes = slice(t * TILE, (t + 1) * TILE)
            kept = block[group(n), lanes] * mask[:, t : t + 1]
            block[group(n), lanes] = kept
            total += kept
            col_sums[:, lanes] += jnp.sum(kept, axis=0, keepdims=True)
        row_sums[:, group(n)] = jnp.sum(total.T, axis=0, keepdims=True)
        return carry

    lax.fori_loop(0, groups, prune, 0)
    to_partner(col_sums, far_sums, sum_sem)
    legs(CHUNKS // 2, CHUNKS)
    lax.fori_loop(0, 8, hop, 0)

    wait(far_sums, sum_sem.at[1])
    shares[col] = row_sums[...] + far_sums[...]

    def share(n, carry):
        other = (col + 1 + n) % SIDE
        pltpu.make_async_remote_copy(
            shares.at[col], shares.at[col], share_send.at[n], share_recv.at[col],
            device_id=row * SIDE + other, device_id_type=LOGICAL,
        ).start()
        return carry

    lax.fori_loop(0, SIDE - 1, share, 0)
    lax.fori_loop(8, 20, hop, 0)

    def share_in(n, carry):
        other = (col + 1 + n) % SIDE
        wait(shares.at[other], share_recv.at[other])
        return carry

    lax.fori_loop(0, SIDE - 1, share_in, 0)
    total = shares[0]
    for n in range(1, SIDE):
        total += shares[n]
    half[...] = 0.5 * total
    to_partner(half, half_far, half_sem)
    lax.fori_loop(20, CHUNKS, hop, 0)

    wait(far_words, word_sem.at[1])
    for t in range(groups):
        tile = row * groups + t
        bits = (far_words[pl.ds(tile // 30, 1), :] >> (tile % 30)) & 1
        far_mask[t : t + 1, :] = bits.astype(jnp.float32)

    def store(n):
        return pltpu.make_async_copy(block.at[:, group(n)], s_out.at[:, group(n)], out_sem.at[n])

    def finish(n, carry):
        wait(arrived.at[group(n)], final_sem.at[n])
        for t in range(groups):
            span = slice(t * TILE, (t + 1) * TILE)
            mirrored = arrived[group(n), span].T * far_mask[t : t + 1, group(n)]
            block[span, group(n)] = 0.5 * (block[span, group(n)] + mirrored)
        store(n).start()
        return carry

    lax.fori_loop(0, groups, finish, 0)
    wait(half_far, half_sem.at[1])
    deg_out[0:1, :] = half[...]
    deg_out[1:2, :] = half_far[...]

    @pl.when(jnp.logical_not(on_diagonal))
    def _():
        def sent(n, carry):
            wait(mid.at[rows(n)], leg_send.at[n])
            return carry

        lax.fori_loop(0, CHUNKS, sent, 0)
        wait(far_words, word_sem.at[0])
        wait(far_sums, sum_sem.at[0])
        wait(half_far, half_sem.at[0])

    def hopped(n, carry):
        _, used = hop_of(n)

        @pl.when(used)
        def _():
            wait(mid.at[rows(n)], hop_send.at[n])

        return carry

    lax.fori_loop(0, CHUNKS, hopped, 0)

    def share_out(n, carry):
        wait(shares.at[col], share_send.at[n])
        return carry

    lax.fori_loop(0, SIDE - 1, share_out, 0)

    def stored(n, carry):
        store(n).wait()
        return carry

    lax.fori_loop(0, groups, stored, 0)


def on_device(affinity, keep_words):
    size, _ = affinity.shape
    groups = size // TILE
    words = jnp.pad(keep_words.T, ((0, 8 - keep_words.shape[1]), (0, 0)))
    vec = pltpu.VMEM((1, size), jnp.float32)
    dma = pltpu.SemaphoreType.DMA
    symmetric, degrees = pl.pallas_call(
        kernel,
        out_shape=(
            jax.ShapeDtypeStruct((size, size), jnp.float32),
            jax.ShapeDtypeStruct((2, size), jnp.float32),
        ),
        in_specs=[pl.BlockSpec(memory_space=pl.ANY), pl.BlockSpec(memory_space=pltpu.VMEM)],
        out_specs=(pl.BlockSpec(memory_space=pl.ANY), pl.BlockSpec(memory_space=pltpu.VMEM)),
        scratch_shapes=[
            pltpu.VMEM((size, size), jnp.float32),
            pltpu.VMEM((size, size), jnp.float32),
            pltpu.VMEM((size, size), jnp.float32),
            pltpu.VMEM((8, size), jnp.int32),
            pltpu.VMEM((groups, size), jnp.float32),
            pltpu.VMEM((groups, size), jnp.float32),
            vec, vec, vec,
            pltpu.VMEM((SIDE, 1, size), jnp.float32),
            vec, vec,
            dma((groups,)), dma((2,)),
            dma((CHUNKS,)), dma((CHUNKS,)), dma((CHUNKS,)), dma((groups,)),
            dma((2,)), dma((SIDE - 1,)), dma((SIDE,)), dma((2,)), dma((groups,)),
        ],
        compiler_params=pltpu.CompilerParams(has_side_effects=True, vmem_limit_bytes=24 << 20),
        name="exchange",
    )(affinity, words)
    total = size * SIDE
    left, right = lax.rsqrt(degrees[0]), lax.rsqrt(degrees[1])
    normalized = total * symmetric * left[:, None] * right[None, :]
    return normalized, degrees[0] / total


def solution(mesh):
    in_specs = (P("row", "col"), P("row", None))
    out_specs = (P("row", "col"), P("row"))
    return jax.shard_map(
        on_device, mesh=mesh, in_specs=in_specs, out_specs=out_specs, check_vma=False
    )
```

time: 280 us -> 184 us (0.66)
  the two profiles are of different devices: /device:TPU:1 before, /device:TPU:80 now
where the time goes in v1:
time: 184 us
  Pallas kernels  177 us (96%)
  other arithmetic  3.02 us (2%)
  local copies, waits for them, and re-layouts  2.95 us (2%)
    pallas_call x1, Pallas kernels, on_device(): pl.pallas_call(kernel, out_shape=(jax.ShapeDtypeStruct((size, size), jnp....  177 us

profile of v1, /device:TPU:80, one launch (start us, length us, event | category | flops | bytes accessed | tf_op | source)
XLA Modules:
  0.0 183.7 jit_solution(15457925351625052283)
XLA Ops:
  0.6 0.8 pad.4.words
  1.4 0.0 copy-start
  1.4 2.2 %copy-done = f32[1024,1024]{1,0:T(8,128)S(1)} copy-done((f32[1024,1024]{1,0:T(8,128)S(1)}, f32[1024,1024]{1,0:T(8,128)}, u32[]{:S(2)}) %copy-start) | copy-done | bytes 4194328
  3.6 177.1 %exchange.1 = (f32[1024,1024]{1,0:T(8,128)S(1)}, f32[2,1024]{1,0:T(2,128)S(1)}) custom-call(f32[1024,1024]{1,0:T(8,128)S(1)} %copy-done, s32[8,1024]{1,0:T(8,128)S(1)} %pad.4.words), custom_call_target="tpu_custom_call" | custom-call | tf_op jit(solution)/shard_map/exchange/pallas_call | solution.py:255
  180.7 0.6 slice_multiply_fusion
  181.3 2.4 %multiply_multiply_fusion = f32[1024,1024]{1,0:T(8,128)} fusion(f32[1024,1024]{1,0:T(8,128)S(1)} %get-tuple-element.4, f32[1024]{0:T(1024)S(1)} %bitcast.5, f32[1024]{0:T(1024)S(1)} %bitcast.6), kind=kLoop, calls=%fused_computation | loop fusion | flops 2097152 | bytes 8396800 | tf_op jit(solution)/shard_map/mul | solution.py:282
Async XLA Ops:
  1.4 2.2 %copy-start = (f32[1024,1024]{1,0:T(8,128)S(1)}, f32[1024,1024]{1,0:T(8,128)}, u32[]{:S(2)}) copy-start(f32[1024,1024]{1,0:T(8,128)} %aff.1) | copy-start | bytes 12582916

commit v2 on v1

--- a/solution.py
+++ b/solution.py
@@ -10,6 +10,8 @@
 TILE = 128
 SIDE = 16
 CHUNKS = 32
+FIRST = 8
+BEFORE_SUMS = 12
 LOGICAL = pl.DeviceIdType.LOGICAL
 OFFSETS = (
     (0, 0), (1, 0), (0, 1), (3, 0), (0, 3), (1, 1), (3, 3), (1, 3),
@@ -27,9 +29,9 @@
 
 
 def kernel(aff, words, s_out, deg_out, block, mid, arrived, far_words, mask_rows, far_mask,
-           col_sums, far_sums, row_sums, shares, half, half_far,
+           col_sums, row_sums, row_shares, col_shares, near, far,
            load_sem, word_sem, leg_send, leg_recv, hop_send, final_sem,
-           sum_sem, share_send, share_recv, half_sem, out_sem):
+           row_send, row_recv, col_send, col_recv, pair_sem, out_sem):
     row = lax.axis_index("row")
     col = lax.axis_index("col")
     me = row * SIDE + col
@@ -121,7 +123,7 @@
 
         return carry
 
-    legs(0, CHUNKS // 2)
+    legs(0, FIRST)
 
     def start_load(n, carry):
         load(n).start()
@@ -157,36 +159,42 @@
         return carry
 
     lax.fori_loop(0, groups, prune, 0)
-    to_partner(col_sums, far_sums, sum_sem)
-    legs(CHUNKS // 2, CHUNKS)
-    lax.fori_loop(0, 8, hop, 0)
-
-    wait(far_sums, sum_sem.at[1])
-    shares[col] = row_sums[...] + far_sums[...]
+    row_shares[col] = row_sums[...]
+    col_shares[row] = col_sums[...]
 
     def share(n, carry):
         other = (col + 1 + n) % SIDE
         pltpu.make_async_remote_copy(
-            shares.at[col], shares.at[col], share_send.at[n], share_recv.at[col],
+            row_shares.at[col], row_shares.at[col], row_send.at[n], row_recv.at[col],
             device_id=row * SIDE + other, device_id_type=LOGICAL,
         ).start()
+        other = (row + 1 + n) % SIDE
+        pltpu.make_async_remote_copy(
+            col_shares.at[row], col_shares.at[row], col_send.at[n], col_recv.at[row],
+            device_id=other * SIDE + col, device_id_type=LOGICAL,
+        ).start()
         return carry
 
     lax.fori_loop(0, SIDE - 1, share, 0)
-    lax.fori_loop(8, 20, hop, 0)
+    legs(FIRST, CHUNKS)
+    lax.fori_loop(0, BEFORE_SUMS, hop, 0)
 
     def share_in(n, carry):
         other = (col + 1 + n) % SIDE
-        wait(shares.at[other], share_recv.at[other])
+        wait(row_shares.at[other], row_recv.at[other])
+        other = (row + 1 + n) % SIDE
+        wait(col_shares.at[other], col_recv.at[other])
         return carry
 
     lax.fori_loop(0, SIDE - 1, share_in, 0)
-    total = shares[0]
+    row_total, col_total = row_shares[0], col_shares[0]
     for n in range(1, SIDE):
-        total += shares[n]
-    half[...] = 0.5 * total
-    to_partner(half, half_far, half_sem)
-    lax.fori_loop(20, CHUNKS, hop, 0)
+        row_total += row_shares[n]
+        col_total += col_shares[n]
+    near[0] = row_total
+    near[1] = col_total
+    to_partner(near, far, pair_sem)
+    lax.fori_loop(BEFORE_SUMS, CHUNKS, hop, 0)
 
     wait(far_words, word_sem.at[1])
     for t in range(groups):
@@ -207,9 +215,9 @@
         return carry
 
     lax.fori_loop(0, groups, finish, 0)
-    wait(half_far, half_sem.at[1])
-    deg_out[0:1, :] = half[...]
-    deg_out[1:2, :] = half_far[...]
+    wait(far, pair_sem.at[1])
+    deg_out[0:1, :] = 0.5 * (near[0] + far[1])
+    deg_out[1:2, :] = 0.5 * (far[0] + near[1])
 
     @pl.when(jnp.logical_not(on_diagonal))
     def _():
@@ -219,8 +227,7 @@
 
         lax.fori_loop(0, CHUNKS, sent, 0)
         wait(far_words, word_sem.at[0])
-        wait(far_sums, sum_sem.at[0])
-        wait(half_far, half_sem.at[0])
+        wait(far, pair_sem.at[0])
 
     def hopped(n, carry):
         _, used = hop_of(n)
@@ -234,7 +241,8 @@
     lax.fori_loop(0, CHUNKS, hopped, 0)
 
     def share_out(n, carry):
-        wait(shares.at[col], share_send.at[n])
+        wait(row_shares.at[col], row_send.at[n])
+        wait(col_shares.at[row], col_send.at[n])
         return carry
 
     lax.fori_loop(0, SIDE - 1, share_out, 0)
@@ -249,7 +257,7 @@
 def on_device(affinity, keep_words):
     size, _ = affinity.shape
     groups = size // TILE
-    words = jnp.pad(keep_words.T, ((0, 8 - keep_words.shape[1]), (0, 0)))
+    words = keep_words.T
     vec = pltpu.VMEM((1, size), jnp.float32)
     dma = pltpu.SemaphoreType.DMA
     symmetric, degrees = pl.pallas_call(
@@ -258,21 +266,23 @@
             jax.ShapeDtypeStruct((size, size), jnp.float32),
             jax.ShapeDtypeStruct((2, size), jnp.float32),
         ),
-        in_specs=[pl.BlockSpec(memory_space=pl.ANY), pl.BlockSpec(memory_space=pltpu.VMEM)],
+        in_specs=[pl.BlockSpec(memory_space=pltpu.HBM), pl.BlockSpec(memory_space=pltpu.VMEM)],
         out_specs=(pl.BlockSpec(memory_space=pl.ANY), pl.BlockSpec(memory_space=pltpu.VMEM)),
         scratch_shapes=[
             pltpu.VMEM((size, size), jnp.float32),
             pltpu.VMEM((size, size), jnp.float32),
             pltpu.VMEM((size, size), jnp.float32),
-            pltpu.VMEM((8, size), jnp.int32),
+            pltpu.VMEM(words.shape, jnp.int32),
             pltpu.VMEM((groups, size), jnp.float32),
             pltpu.VMEM((groups, size), jnp.float32),
-            vec, vec, vec,
+            vec, vec,
             pltpu.VMEM((SIDE, 1, size), jnp.float32),
-            vec, vec,
+            pltpu.VMEM((SIDE, 1, size), jnp.float32),
+            pltpu.VMEM((2, 1, size), jnp.float32),
+            pltpu.VMEM((2, 1, size), jnp.float32),
             dma((groups,)), dma((2,)),
             dma((CHUNKS,)), dma((CHUNKS,)), dma((CHUNKS,)), dma((groups,)),
-            dma((2,)), dma((SIDE - 1,)), dma((SIDE,)), dma((2,)), dma((groups,)),
+            dma((SIDE - 1,)), dma((SIDE,)), dma((SIDE - 1,)), dma((SIDE,)), dma((2,)), dma((groups,)),
         ],
         compiler_params=pltpu.CompilerParams(has_side_effects=True, vmem_limit_bytes=24 << 20),
         name="exchange",

time: 184 us -> 166 us (0.902)
  the two profiles are of different devices: /device:TPU:80 before, /device:TPU:185 now
where the time goes in v2:
time: 166 us
  Pallas kernels  159 us (96%)
  other arithmetic  3.02 us (2%)
  local copies, waits for them, and re-layouts  2.94 us (2%)
    pallas_call x1, Pallas kernels, on_device(): pl.pallas_call(kernel, out_shape=(jax.ShapeDtypeStruct((size, size), jnp....  159 us

profile of v2, /device:TPU:185, one launch (start us, length us, event | category | flops | bytes accessed | tf_op | source)
XLA Modules:
  0.0 165.7 jit_solution(15984994353543593906)
XLA Ops:
  0.6 0.0 copy-start
  0.6 2.2 %copy-done = f32[1024,1024]{1,0:T(8,128)S(1)} copy-done((f32[1024,1024]{1,0:T(8,128)S(1)}, f32[1024,1024]{1,0:T(8,128)}, u32[]{:S(2)}) %copy-start) | copy-done | bytes 4194328
  2.8 0.0 copy-start.1
  2.8 0.8 copy-done.1
  3.6 159.1 %exchange.1 = (f32[1024,1024]{1,0:T(8,128)S(1)}, f32[2,1024]{1,0:T(2,128)S(1)}) custom-call(f32[1024,1024]{1,0:T(8,128)S(1)} %copy-done, s32[5,1024]{1,0:T(8,128)S(1)} %bitcast.4), custom_call_target="tpu_custom_call" | custom-call | tf_op jit(solution)/shard_map/exchange/pallas_call | solution.py:263
  162.7 0.6 slice_multiply_fusion
  163.3 2.4 %multiply_multiply_fusion = f32[1024,1024]{1,0:T(8,128)} fusion(f32[1024,1024]{1,0:T(8,128)S(1)} %get-tuple-element.4, f32[1024]{0:T(1024)S(1)} %bitcast.5, f32[1024]{0:T(1024)S(1)} %bitcast.6), kind=kLoop, calls=%fused_computation | loop fusion | flops 2097152 | bytes 8396800 | tf_op jit(solution)/shard_map/mul | solution.py:292
Async XLA Ops:
  0.6 2.2 %copy-start = (f32[1024,1024]{1,0:T(8,128)S(1)}, f32[1024,1024]{1,0:T(8,128)}, u32[]{:S(2)}) copy-start(f32[1024,1024]{1,0:T(8,128)} %aff.1) | copy-start | bytes 12582916
  2.8 0.8 copy-start.1

commit v3 on v2

--- a/solution.py
+++ b/solution.py
@@ -13,22 +13,279 @@
 FIRST = 8
 BEFORE_SUMS = 12
 LOGICAL = pl.DeviceIdType.LOGICAL
-OFFSETS = (
-    (0, 0), (1, 0), (0, 1), (3, 0), (0, 3), (1, 1), (3, 3), (1, 3),
-    (3, 1), (2, 0), (0, 2), (2, 1), (1, 2), (2, 3), (3, 2), (2, 2),
+DIRECT = 127
+MAX_RELAYED = 114
+SENDS = (
+    0x1fff07bf83bfc1cfe0dff06bf833fc18fe0bff05bf82bfc14fe09ff04bf823fc10fe07ff03bf81bfc0cfe05ff02bf813fc08fe03ff01bf80bfc04fe01ff00bf803fc00fe0,
+    0x1fff07bf83bfc1cfe0dff06bf833fc18fe0bff05bf82bfc14fe097f04d2563fc0ffe0820abbf81bfc0cfe05ff02bf813fc08fe03ff01bf80bfc04fe01ff00bf803fc00fe0,
+    0x171219bf83cb83d561e290ed3074902206458f180093284383e1b9d0d8d85844d52e1a160a460ce2c732619100c4706030251031861bc505a243f06e50508420d00824001,
+    0x1fff07bf83bfc12373e7f06ff820627afe0cff03cbcf1fc0d2d3bff05bf8184e630745119a46cc40a95fe0a7f04ff8000691fe077f01c5cd7fc0613347f017f8021264fe0,
+    0x1ff107b803bb81cd80dea06b40339418c60be105b002b7814b809da04ac0235410a607d003a601b1c0b860542025e810dc07640600299700a9c0448019a008a0024400180,
+    0x1fff07bf83bfc1cfe0dff06bf833fc18fe0bff05bf82bfc14fe09ff04bf823fc10fe07ff03bf81bfc0cfe05ff02bf813fc08fe03ff01bf80bfc04fe01ff00bf803fc00fe0,
+    0x15024fa18be09a6029ec116519b801b6426dbc117f834e8586e2bb515598a8c4535e292c14558a0a44f4e2724104025a844c3e259b124a88e4042fe040931040861440002,
+    0x1eff07c36f9fc132b2dff06bf833fc17fe071195bf81a3655fe0c05ed3f8040e6a1528ff0781421fc091327ff01c348832e509267f04807460a4bfe0003ba3f8020246fe0,
+    0x1882564807a846afe0e1e1ecd8ee3c3a323182354707058721813ff058a0e840731a308033c50602c6e10327f03448561c2614c6051a0287e248208c2830a408fc1080020,
+    0x1fff07bf80e3b3dfe0792b73f837fc1afe0300f348db3fc18fe0bff05bf82bfc0b216a7f04ff825fc11fe01988c3f8123acefe067f02bf80bfc04fe040cb0bf8000b41fe0,
+    0x1fff07bf83bfc1cfe0dff06bf833fc18fe0bff05bf82bfc14fe09ff04bf823fc10fe07ff03bf81bfc0cfe05ff02bf813fc08fe03ff01bf80bfc04fe01ff00bf803fc00fe0,
+    0x1fff07bf83bfc1cfe0dff06bf833fc18fe0bff05bf8020354fe09ff04bf823fc10fe07ff03bf81bfc0cfe05ff02bf813fc07fe037f017f809fc03fe017f0542fd062e0fe0,
+    0x12ff07c39f2ad8a0ab17f02022f7341a960c4805e30383d16800abb050fb22659368092f041601ea40e4c06a100c1bd87c0b3a0f043a4c80e5c0626020e07401c22c000a0,
+    0x1f8dbe45dec2af3117f508f674601efc991dc98ea34710e2d0d7605bddf468e22709792f8c55c5e9e2e4115928a816d2422303040e89405cc3224131aff0083c421220031,
+    0x1ecd17ca9f9305b962d4a16648b120578e2f1855a30ab10548429c0149f0a2ec507227b61399084016d60262e12d5094a0494c242310403ce80463a229811098864440022,
+    0x1fff07bf83bfc1cfe0dff06bf833fc18fe0bff05bf82bfc14fe09ff04bf823fc10fe07ff03bf81bfc0cfe05ff02bf813fc08fe03ff01bf80bfc04fe01ff00bf803fc00fe0,
+    0x1fff07bf83bfc1cfe0dff06bf833fc18fe0bff05bf82bfc14fe09ff04bf823fc10fe07ff03bf81bfc0cfe05ff02bf80600800ec4ff023f80ffc06fe02ff013f805fc01fe0,
+    0x1c7f05bf829fc0101cf958f89c7a4a33fe097f0708c63fc1b1d187f03ff834362efe06ff033f815fc0b1f94ff023f80ffc190f137f05c1c49fc150311ff00bf801fc05015,
+    0x1f9767bf83a598c126700270ab3651930c248c7689b102dd924cc116104bae41961ec38310c3baa39941ac90c6445b20298f12c084734430a052b0ec5066181b0009c200c,
+    0x1508db4b5fe639e2fce96e706636579a29cc93e60972eba7623ca10e4c7f243b911bc80ce3c5f1c2b8c13c595b9c470a1f8843f48ac1907c81b830bc104e041f000395573,
+    0x19044fca037059a78c8034e5d330d9961adbb56558328b59150c98b6bd2b1c818d10d5866a7f81411a604d61e6785010498302d38d613f83a18050cc1006842338040000c,
+    0x1690aa4654c12b8fe0a7f0718659fc0afe02ff07e177d03bd7bddbbe8ff834e7b96ddbb4ed99743fc1561d9acec90e62a3b049d7a1eb8ef566ba82fd393e88574806a005d,
+    0x14032d8d8aa645e069fb56f5a378cda5fe0a1816d8b74c1b95ad99611d13b0a9b750d8256c8a0a24c4f2027226b5035471ac1c2319690a3562c431ed10b68443521c4008d,
+    0x1787dfd54fca27d4f3703cf12cf6927a453ca198807707e773d3b1c9a487941b75353a179ccb4cc33d22938929c08cda426c1f320bf2c6cc623c81733889943cc20a60013,
+    0x1f8d57862ba2d5a261c920f0528c01d8221b900d8786a21541c19875486862195018178b0b42a9c282c1215845241a94202804a387094304614220612015001076000100a,
+    0x19ff07c95a5fc1e2368ff074859ffc0efe06ff0707db63accfe0d0db2ff83232c9fe047f0605d8dfc171562ff0584d89fc1511617f007f8281ad00b6504b1c1d8602c0fe0,
+    0x168c52c5a85fc0e3cef9f378f1ba74c812ae1c307f8125ddb366d1a364c9b05cd72c6b15354a18e49d426699234889a240d01e678e3106b9830ca166308314398608c0fe0,
+    0x1583b5496bed3c4056f33f759784127c63edb0f697f8206795dec2df5d67acafd455e9a9f0005e4a3d14fe826f3d279c8fcd43e620f28f79273c837e399f18b78a4bc30fe,
+    0x1f8a3b842fa24fefe0dff063f82ffc16fe0aff0343ae9fc13fe06065f041e5fc1a0e75045c7f80c09790c787f03ff80e0ce502b2023aff813fc08fe017f007f80604e0fe0,
+    0x1d05bd425fe477e21b409af47ef83b7b1bb883b900df2337817bb8add84ee82360017507b4c4c581f6b0db485dc844601a2e0df384d981eca0b6f091085e8c0eda022201b,
+    0x1101568cafed9fe6afeb47f19bf6c9f962fc307dd7becb9f55afa2c7cd53e4a5f14ef8105bd2bdc8ded42f6207acebd46de932f41779cabcc45e51af20978c2bc209e000f,
+    0x1f9dbf8e5fa6ee4fe0e1abeccdf462f92f7c14bdc9dec4af523771afaca7e842e921f1ff04c7de43ae615f88dbc065de2eed157608b9437c40be1fe0507ba025c003e7057,
+    0x1fbf20ff829bd1e7c4ebd26de134ec9974417f061c92ee0966c4e03655a926d0926640ff0459101fc106247b0239791ab88cac85ad2296112a8884e43a5219110a4084308,
+    0x1d14f78e47a6e3c351c9989016304fd62f1a1688c05368eb7415a9eacca4602bd1315708f34ad643e21fe0613abcce4e3aa5195486888457e2ba80b1303883f81607ca01e,
+    0x1281204013a60ff04ce173bc2b8814de00cd963e8a9f250f826749655c91ec44e2086a8f3d071ce39531a790c3c459e028e314a7093b441d818eb0a700652819d1fc06047,
+    0x1a0ba484d0ffc11114e09bf8f4fab77b59bd2ade546f09b774bbb24dbc3d181a9547b505a4d16d0128507481fd8c151c7b6d3bb59cda4cec206862bb212dfc07043f60014,
+    0x1f0a7fca0324c09fe04022cc702e8484fe0b20254e1286881fe0918244b90c04b02a4794208015c489d12f68f27043d8389b0cf58b2682bd4248710428520c193009e0004,
+    0x127f00ff805fc1ba590ff003f83d12bd875e42aea0d7302b87f5bbdad9dd6ae6b46f59b4ac98d62bab05b57abab94d7e5fad515626aad2d5472a9355419a9cb54c12a5035,
+    0x1e1137d927cbd3a206eac4e479b69d371c6aa34d069a079388aa71a4d9faa6f54c309938545a294552f5aa3124948a4835281a26a55043a4e28cb38a18830839926940069,
+    0x1e14b7bf83e12ad05518cdec9d9012e6077d11b0815f242d81f6b8eb002ed427f61b6081a942fea32d417698ab77f82426d1116807b3c359c16cc096583b24158e06c4016,
+    0x1e890fbf8382036120f8934c40344c8c02eb96650ab244d9124c7916387b1639891ac38c6185b361c390c12886103b15fc030acc050d42044211006100263410500421001,
+    0x19a6efcafa497be1fe8a3ec1177a37cf43d69feb0f75677bc17e51cea4df506bb6311d89f1ccf6a562631dd07f509c721bc52dd214edc2fb1fc031fd7088885f4217a005d,
+    0x167f02ff813fc08fe02ff00ff803fc1e52eea87713bb499d94aec2475d13ac81d53eea1e74ceba471c0fe089a740bbb7394f2ae7127347b9431df246388718238809c200e,
+    0x1cb6d63f83e4fde25eaff0748f9ffc1c21ed8ff6877ac37d419e98bf48579dfc1113e808f33f81a1fcb0debb5d242f9013cafe0383f1bf809fc0505e17f00c0f81fc0101e,
+    0x1f853bf22000dfefe0ab726d3b3299974aca246491b22898108b8216350338600c3ecd17060b016798a3ac9a9224e33a00f624041b638680e6985180319610c30628022ec,
+    0x1f90fe0947c3ffd1df905db426f833eb07b482dd876aa375419a301dcc5eb627fa07f41ecbc4eae2e3905f708d303e941b510f1385d400fca134407a102d040e86036001a,
+    0x1f947e3f83c4df1fe067f04c18ba49fc22fd907a7f8343df91cfb8d79bf82c31f516fa0a7c84bde21e4fe06877ac33c5fc0a0af801107f801fc0e00240479c1bca09e302f,
+    0x197f075e7f8effb75f37f00ff834e7f971fc37f8bf82edbf66bfab4ffc55e8cff365f8b1fc187debfee5bf6acfb14ffc02eb4df523f840ed283e83bf39bf94afc1fc041df,
+    0x1a0b64ff825fc11fe0787643f81dfc0d0ccfed22c2b19fc1ed64ee922423399c8afe030366f31080988fe0d6221ff80bfc0202ccdf262e907fc17b64b59207f82b5c80fe0,
+    0x1f89a78451c0f1007ce48a8ff83a1e9a8f5c44ada0d761a8d05cabfacde564eab16b5c85a3d75589aab475501e2016126ea6038280c106d6e12820d5380e041d680e80015,
+    0x191c3fc723c351d188a87190126268f0307e0b438291610830297963ec521a50f4083d0943099f2210a207c0742071d208970c8b016180926046100938540819ca1100027,
+    0x1dff0702616677afe0e86e63f82ffc16fe0aff053f827fc12fe08ff0780d21fc0ffe077f07c2ff20fe20db6ff033f815fc09fe047f01ff80dfc05fe027f00ff803fc00fe0,
+    0x13844f2a131fc1e480f91674f02dfc14fe0dd226a89333c97944ac524df923fc127247ff041991bfc0bfe02014b959188c89fe051c220b10a4086fe018a2001905fc01fe0,
+    0x1f91eb3f8322bbea3557f0767d7936bb975d4aae22d47fc176f5b33ad58d68b6a0fe09aaac94d6096af455690cb8fd5672a82d5395a98a54a46a41f548cc885d620ba1115,
+    0x16034f3f837fc1afe0cff05bf82bfc14fe09ff047f81ffc1814e4993483356354714a77f023f83e1844fe029430bf8063cd70ce6862c02b7c0841fe03012a82341fc1d002,
+    0x1f05cc475fe27e727bc05e5c2719fc0b117a85ef0264c16ca0f7703e2017060ec2036d83c900f0bfc00fe0a04ed81642039d075d02ae40d660fb2039780cc0175a07a901d,
+    0x1f8174d402c55914c0ea63f803b894fb487d233e511f080f73e7a9d3d0e1e468f03077973b8a9da4cec2475913a879d238e818718131c51cc24e50e720638819c208e0007,
+    0x180deb426940f4105afa8b793db89adb4b6d24b651db08ad7436b20b54fda87ad33b691cb44dd9e6ace336618b2cbd925add03e415b1ca58c4ec5256211b0c85843ec0156,
+    0x1fff07bf83bfc1cfe0dff06bf833fc18fe0bff05bf82bfc14fe09ff04bf823fc0b0ae87f03ff81dfc0dfe067f02bf813fc08fe03ff01bf80bfc04fe01ff00bf803fc00fe0,
+    0x1f7f077f837fc1afe0ca5b5bf829fc12fe0c22b43f81bfc0cfe0a9fb7c0cd5fc0015b99db44d591fc0f31637f05c0ff807ce2f627f02ca5924ec71f61ff00bf80a3ac1fe0,
+    0x1d2306c833274183609ce242492e580e88463e229c12c440920843121d512a341e527ea83d0600c888102b29b2483808548f0c018f247f81a080212458107139fe01e0044,
+    0x1fbe8f9e47aea3c711db68e9ac72ce38651baf8d9646aaa344f19a48c914627e303b179b8b8bc5a522c2515918a88452362817138a8984c4a1e240d11858881c420a20011,
+    0x1dff06bf83eacf8fe0b7f057f827fc1e50770474bf823fc1d4c787f03ff83890edfe067f06511c6016bfe057f05cf9e878e102a003327f80ffc0814737f013f80a1ce2fe0,
+    0x1fff07bf83bfc1cfe0dff06bf833fc18fe0b7f057f827fc12fe08ff043f81dfc0dfe067f02ff815fc09fe0babba3f80ffc1453737f017f809fc03fe07a7b8bf803fc00fe0,
+    0x1fff07bf83bfc1cfe0dff06bf833fc18fe0bff05bf82bfc14fe09ff04bf823fc10fe07ff03bf81bfc0cfe05ff02bf813fc08fe03ff01bf80bfc04fe01ff00bf803fc00fe0,
+    0x1f7f077f839fc1bfe0d7f067f831fc17fe0b7f057f829fc13fe08ff043f83ea32ffe077f037f819fc1239d5ff02bf813fc08fe03ff01bf80bfc04fe01ff00bf803fc00fe0,
+    0x1fa20f9007a783c381d1a0e4c04e48782c1d8d6dc986c4835221a1009878e63c251631881c8706230220c378a090221c202808d6860c0031810210835830a808400869001,
+    0x1eff06bf8300380014bff05bf83e967e473aff0710cf67e74fe097f064f4e1fc1337389a9b8bcd65a692933129bff81bfc051f367f01064d5fc0313347f00834cffc01033,
+    0x1fcd07a603b2c1c940dc906a40331c188c0bc50562029081382093f045f02ca990760739035b818d00f6045b00297812b4085603a9019380a900444019e008d8025000020,
+    0x1fff07bf83bfc1cfe0dff06bf833fc18fe0bff05bf82bfc14fe09ff04bf823fc10fe07ff03bf81bfc0cfe05ff02bf813fc08fe03ff01bf80bfc04fe01ff00bf803fc00fe0,
+    0x1dff06bf83ce45c6a2cb1163f82cb854562928141289c845f10d69f15ff8167055fe09ff024c8ba19a72828ff0148088384ffe018b1083899fc0afe047f004188c0520022,
+    0x1eae97c5778b65e13dd2b96554b0a65b11dba79592ca61fb5472a21944f49e6a4e2f2906eb09ca017a001357f03427560fa9252302ea0848e324301d2899102c840a41012,
+    0x181001812a4798100af924389b3c391d341509070c856359b301d170e0b06e5436281a930d0906644311e1388608019e34240a068b0b048521c390e4000020284a0c23021,
+    0x1fff07bf83bfc1cfe0dff0042775fc19fe0c7f05ff82dfc15fe0a7f04ff825fc11fe087f03ff81dfc0dfe067f02ff815fc09fe047f01ff80dfc05fe027f00ff805fc00fe0,
+    0x1fff07bf83bfc1cfe0dff06bf833fc18fe0bff05bf82bfc14fe09ff04bf823fc10fe07ff03bf81bfc0cfe05ff02bf813fc08fe03ff01bf80bfc04fe01ff00bf803fc00fe0,
+    0x1fff07bf83bfc1cfe0dff06bf833fc18fe0bff05bf82bfc14fe09ff04bf81612d1fe087f03ff81dfc0dfe067f02bf813fc08fe03ff01bf80bfc04fe01ff00bf803fc00fe0,
+    0x1f7f077f839fc1bfe0d7f067f831fc17fe0b7f057f81405f4fe09ff04bf83e3111fe087f03ff81dfc0dfe067f02ff813fc08fe03ff01bf80bfc04fe01ff00bf803fc00fe0,
+    0x11ff0781cbe03e0051eb582c3678ce01fe0db28698432ba18590baa8593c2a9a144909a2848fc227a1039079b838cc1a620c2d0515824941042071d030c81454081e02070,
+    0x1f5417690b9405b9e2d4d16660b12857922b4715630a9105382293e145e0a0e84f6c27321357898b04b522526125189080473a231a114a88848431421091043080145f086,
+    0x1fff07bf83bfc1cfe0dff06bf833fc18fe0bff05bf82bfc14fe09ff04bf823fc10fe07ff03bf81bfc0cfe05ff02bf813fc08fe03ff01bf80bfc04fe01ff00bf803fc00fe0,
+    0x1f7f077f83e149cfe0dff06bf833fc101ecc7f02c5b2ffc040ec08145bf82bfc14fe09ff04bf823fc0ffe077f037f819fc0208c57f027f811fc07fe037f017f807fc00fe0,
+    0x1403c14160ffc04fe0fa2abcd67c6eae2b9d38e65bf184b376dc92fe07f816432a199100c455f1a029047ce8d8f06452279b151c088982f2c162305ca838d00c400393011,
+    0x1f9c1b42b3c686b08ce981f0b0d00d9b2a3b247e498f0447720391d7d470e8307032f98a1c448f5fc0c2af30260c0b1e1c6a28f7051a418ce41e51cf202180030229e2023,
+    0x1d81a084dc21aff49cf23e75173883993dcc1ce5cd72c67952fca15e4c9f244b9121c80fe3c771c378d19c60be2c57002fea13cd00a2447101f870dc305e1427080f8305c,
+    0x108049ff81a41bf2842ff02c735e719e520ea7030c238941b44050c6e8f8327018340b97024536c4c0810d3066d48028380408d98c00ff8242011080802008134001ae000,
+    0x1fff07bf83bfc1cfe0dff06bf833fc18fe0bff05bf82bfc14fe09ff0001665fc11fe087f03ff81dfc0dfe067f02ff815fc09fe047f01ff80dfc05fe027f00ff805fc01fe0,
+    0x1fb1139a3bcbc5d5a2e2c16d509448da4e232476528a085b8462ba213cfb6245563e261d6d4e8966da12eea1a14cb8a4504832d69011cbb4855a328d48c514388025a2022,
+    0x160b927f83e6fbe35de99ef0c7765fba2ddc95ed824f053ab13250795c9f501a5525d208f9c2c8c0a5423d990ec87f623bb01bd185f8427de33a20bb70beb4574a0240039,
+    0x1582703f81005c306a10257cd90801de2e408057520f88c7b423d1f1e4e8f07077343b181d4b0e850732639111c470e0346f1637091b440d8186a0a348419c18cc0465003,
+    0x1aff04bf83e3f5e1da87f03bf81bfc1d1bae0cd5025762f4cfe057f027f8342b58056c89d5c468dfc160fa986d442e9e134b07a402d0ff80e06c503a17f0100581fc0101a,
+    0x198d57eabbd4dc7fe0ed177273b72dda90ecc5762139c21577aeb3775583a8b5d254e8a77411396194f3ce37f034db9861c922e40f714638821ca06a17f003f80611c104e,
+    0x1fb5f4406bcd3dd67ee32f48a5f6c7da61e78ebe57fb0b3d751e70bbd937985b690b7aa4f1c76c5fc08097a22f4ce7882365077819f34af963fca17e307f0c1f8007c1017,
+    0x107f02411e47d9f0cbe8559009e0699b08b7986714014691a4c069566518184d8b24c41165ce80e39851ac30e458b0300d6e04b18a6548804219e104a0904c28020d91020,
+    0x1486ffc0ecdfc1e197514ef45dce03fc1572ff020977626f91b2c0c96845ec2a570f798995435e41e510d2a05bb82ca012ed0520ff03c1dd806430bd202bac048402e003d,
+    0x1fb37f993fac5fb60fd2f7e573eeb5f558f9ab78ff80e4ddc3029287e0b0ac48542228267b90bc5fc111e278b134f3d82441fe050512cd3d25de806228c7903bcc004000f,
+    0x1fb5ff5a7f6cff965fbb0ffbf82abffc3fbd7f05bf826b7edfe092cfabf822afe6fe02ff03d57dca7ec51fc1ddd0dec7fc0b4ff817ba537c5fc0845f0ff01ce7c1fc041df,
+    0x1daf22ff83ee59a5c427f079c332b482fe0eb6661612eac96524aa8251392698924a48a4241191e8880fe0721234f9186c9c6ac51422489103c8718430a21431061081004,
+    0x1f988f0ad36529a274c12a5c8d3c4bbd2d1b10a649c683e9523198ea446d243e2e19480c8b05d142a8f151489a1c450a1e8d111186a2c3c4416880b1084a000d0c0a24011,
+    0x1d8e3a028be1c9a1a7c9035c61f03cd4167f0624c51e024f61c66883f429242ccc0e75063bc51b810821aa70932429ea39c508788321019c0044b0e630221c298608c1024,
+    0x1f8ea786d2c96fd194a24bcd1df62e91457d0aa48d4e0666f437720be04d2e228d3d761cbacc4d25a6a357cff01c94ea1e851f3301c1064c00688337197b8806380781277,
+    0x1f132f4917844bb20577f033f8323cb71c5b0d2abf82830b216588a2c049741809fe0c0403c415a1cab0c54052fc034ffc0608520328c114bfc1504017f00409660000fe0,
+    0x1fb6af9ad74a327fe027f0653e45fc1d6950ff0719d76cab7635ab0acd7d64bab15b5c26cc16541fc0f57572aab54d6c972c4d55a3aa8fd5262a81f5a24c984d4a1ea3075,
+    0x128d4fd2095fc1e462ea217108b6805a3e220b4e4f0b07457382b1b154d0a864533021852c8b8a258502a21074bca09c4c4d22260f12c708215291820024a0508e20460c2,
+    0x1310dec37fe2bbe11de87eb84e5a232c0f9586ce42fd41728099b83fe85d8e0f38156b09b5445a81ec3053986b482da212c1033003dc01db80faf056282c900e5206c2019,
+    0x1202779ba7ad13c629dae4d10319fc1a56999e644db1c6599529c264dd1a56618202eb214a4ab0e499540991f4987b2079251ac18a63cea42198d389f81328da400d88fe0,
+    0x1b7f07d3f70434517ef26ef52f50335c49dda3e905eb48bb943daa0ed0ff667ba309e89dec91e440fcf39d71bec1165a6ba10baba38b0cf5663a003a517ea4b74e57a629d,
+    0x1a43575b38bfc04fe094053dfab8d5db68e73b50ff834cdcc70acb277c99b0c1ca66abae707f82cadd552e9a874533a091cd42ef12303f81679c936e41971cab8c21c204e,
+    0x1b14f486581fc1e2b3a13f4c97a247cf21ed939e48cea834c1deb909b86cd637df0d480bfa86788226915e1879a047ba168d13f308f9c1f8a07c20ffe04a681d300a8101f,
+    0x1fa27f903f6d19a66c99e7e193226def32fbb1630bbd455e924f3907f1aa32c5165ecaae6187bda95145ac20c7f401c629f258c4204043bc4096004f82a614b21c918b42c,
+    0x1d84e389f7e2b7807c693ce407fc1f7d698511ecc2ed243a81fd38eef18e34b71751828bed92e0827a30fda81e5106220386fe0817c3c9e041ba109d60fc4826c00bab05b,
+    0x1c9f7d0ebf4405236f8977fc7170345028f07f058589e49f51229871307bfc30bd165e0a2ec495635f70e53831205bc6084d1ae2887b8194819e208f5022a4094201e6005,
+    0x127f07cffd626e8097ab1d8ff83c7be2fe00ff074eff873fb37f07f068d7e8bb7933fc18fdcbfec5bf32bf914fc49fe04bef23f710fb47fd83bea1bf319da467ca0be7017,
+    0x1fa0617f809fc1e3ec17f072193a7994748dc0249ba347181fe0cbd25de12ce8957049b62459920c88f5c472c2355118a08b4c45232250910749832c399218b90630800c4,
+    0x1e82e7d4451fc1e4f1e01e1bf834a699058aa1a48ed3682b0354c1eadced6c72b437599aac4cd5e5eae2d51ff0348d583eab1d550daa45d4e26a5115101a103d4212a0015,
+    0x1eff07c6b3c319816ce7f02410f7fc1614cd7f0504b33fc1210cbff057f8201d8702370664ff823fc0ffe0605637f80c0d8bfe020262bf811fc02fe018161400c20180fe0,
+    0x1f21a43f83a7e8ffe0e1da6cdd1bfc1a31467f02bf8325a89fe03ff05ca50dfc04fe01ff00bf83e6301fe007f0149dd02bf5234c149d894e8467321390d9c45cdc1a6b033,
+    0x1f9d674d32a619e705896671b15e559b6a5d332e5915c4d9860561165d795441965a540f61c6b28b0a616c9aa2945324a0a412c82728c3b1a94a20405a42841b1288a002c,
+    0x1fafef9777ab7bc59d0ff06d5f74abb953dc27edd376c97b549da21ecd07647fb03dd79deb8e75a6bb1435619eacbf5457a929d412e9c874c3ba51bd20be8c4f440fa003d,
+    0x1b896d84359fc0600ea876fc527c253d10950652ff813fc1c0e947f01ff836193a0a92ff0503349fc120adc844c02345fc180699824c40a5c0da10066826bc0241fc0300d,
+    0x1d89cac07721b360b9f97c78b63a571c298d13c60962e471221888fc407607fc1509978dc3866182f0a158489c2046280b270f8306c142e081302078981c83f8020b0d019,
+    0x129440c28040c1f06af19374c1b85cdb2c6d15364a1b04cd7246b113540ba840d31e688e33c699c30cd16660a34bf81624d0fe008b428418008890e640631c298c10c4066,
+    0x1ea58d4fd78923b451d218fc7eb282383d1b9d8d8dc5862b43319978c8b45456b129181389c855e462e1d168d89065562a221554888a0347c3b460b1086a940c400ea3011,
+    0x1fff07bf83bfc1cfe0dff06bf833fc18fe0bff05bf82bfc14fe09ff04bf823fc10fe07ff03bf81bfc0cfe05ff02bf813fc08fe03ff01bf809fc03fe017f007f801fc0518a,
+    0x1c1fb7cc4e5fc163b6f159c7f81ffc0823730dbf47cea6ed41fa998b37f819fc102d6714b7064d3fc0b236d8a9a87587fc1a0f338db1455b20e64116106b5c14c20760096,
+    0x1e913fd003440fe3a0c0f3d871f8701b320c9705469e830f32c0bff044a8202cef1471807b4901640125687093b041d21cea1603063a0480a14e408710338409ce1c00007,
+    0x1c12b7c0efc3af7236894a746dec3ecf234a8eb7065da368503fa0db6c5de42e3311a70ab305d3426eb136408a2845b222e90f6306a1c35a00ee2094184b04158002c4037,
+    0x121635102b081753cb0ff044e2964d5c547da93e939de65794a7ba33d911e680f23e781c3b8d9da60ec2c748472899d044e61a7f8411449ce295e022e8010c29c40ce0027,
+    0x1e7f06ff835fc18fe0bff05bf82bfc1f497f20bd3f83a76f2fe08ff04cc5e1fc0ffe06ff033f817fc0afe0715ba7f8322b64157107ba3f80ffc0005737f017f807fc01fe0,
 )
-
-
-def packed(values):
-    word = sum(v << (2 * n) for n, v in enumerate(values))
-    return word - (1 << 32) if word >= 1 << 31 else word
-
-
-X_STEPS = packed([o[0] for o in OFFSETS])
-Y_STEPS = packed([o[1] for o in OFFSETS])
-
-
-def kernel(aff, words, s_out, deg_out, block, mid, arrived, far_words, mask_rows, far_mask,
+RELAYS = (
+    0x1f87c1a23a1fb381f3361eb341e336cc85ebc074cb86c1cb2a1c3281bb261b3241ab1888878d8076dd35e1cb66fd8dc1d0eed83f03686e3ab5cf58541d96c39b58f48745a8f259354f40705b9663834e143ea590cc1a1603734ef78e25285c379481634cf68dc560d8558d4d2bc6148c8838d0d23c4130d05084ad1bc833940108c6d13c4a010a500c250340f00805,
+    0x1ff3dcef37ccf2fca70981cc34,
+    0x1f93a4e1364d1324c12e4b12a4a124489204791a4591447316c3112c33044,
+    0x7f4f53b4dd354cd314b52949d2548d2147d1d4650f42d0941d0540d3d1f7014,
+    0x722b8aa2b1642995e2689a55896540945288c519445,
+    0x779f77d3ef7b3e7793df75ddcf9cd7353c771cc4ff5b73d5af2f3ed67cdd65cd5693bf7358f2f5b76d5af6b594dfca76758ce7d976357cd9c876155f1fd7d5d37751b7557d4f1757e0724551d3f4dd3d5732f53327513270d31745524c3d14c5c0dc330f01504c1c,
+    0x1f97a5e17e9d9745f27c0c97a9e8305e02e5da76081740aa5c5c81a5c0209b8145b01c931589a828052485980c92a6401962022600115e0680250a5ad500050250033480,
+    0x1ef75dcf455,
+    0x11b8c6,
+    0x7fef7b9edfb5ecfb1ebfadeafa9e9fa5e8f9fe7799e5f93e478fe378be2787e17adbaee9b9ec1e7eddb66d5b3ecbb26c5b0ec1b,
+    0x76ae8f83d8f43c8f03b8ec3c26a3f0683e8663b26439a76188f4180e49c05e3b8629a85c3a05a3985837a6418856380543785236a5c140ce5684e3605c630d69585294b4a349928484ad20ce618ce11b4e8219244106821081190081842403c0400c01,
+    0x73abebf6f5bb6e5b76d5b36c5af6b5a969da568da16cf9f675b1e6d996af9569f93645a3e3d9fe778d69c57e4f8b6745353f8be6c4d5255514c4751d8f1374b11f47117431,
+    0x1f3fafe3faee3b6ed3b2ee8b0ebbb82aba8ed8a4ed0a0e7bb0273ac26b98e5ba825392e9890e808ee339c22b88e6082b1382e4880e,
+    0x5d796dbb5ed3b36c7b,
+    0x7e7f1fa7e1f67c9f07b9ec7a9e87fbe6791fcf89faf79f8f71f2f69d87bbe8f59e4c51e2c49e0c41dec39dac631c031d4c5810c29d203810f21ca02bc6019c201302703007,
+    0x1ee378bff58a7f387ff18be2d8ae278450d4861d86e178941d74e2107c1b03617764098541371623d4c0793c0d73417d574b706430144570ec17,
+    0x1d9f27b9e8791e2781da761d6751d2741ce731c8711ee6a1be191a267992b71966498e631bc1fb8a621ba119bcee1006e0762,
+    0x176118360b8,
+    0x7e8f23a8e2368d2328c22e83a0a8133e4033c4,
+    0x7981f05c073f4,
+    0x1d0b22c0ae2b0a8290a02789c260942388a2188e9108022258d,
+    0x67695a7c8da167da1c6d9965d9564d9163d8d6fd4b6fc096f43b0e41b91db70d413915bf49ce53cc2130d9f3bc016ac1b3,
+    0x1624881a028,
+    0x1f6799de6d9965f9,
+    0x46e6182e,
+    0x1fdb54c51fe6f97ef593eed91ee5a14dd9d4d5b36bd9ba5683a5d154,
+    0x1f1ba6e1b46c9b06cb6e6b36c6a9a8699a46b0626a868181a6179a41885c6631e1699815a546584e9434e648660790c6380860ac46,
+    0x1fdbd6edb96ddb56b5a969da568da166d9764d9163d8b61d836,
+    0x7c5e9785fbf65d17cf01f050afaf,
+    0x7f7f5fb7fff97cfedfdde7f87dbf67cffd5f3785cbf,
+    0x1fbfe7f1fa7e1f67d1f27b9ec7a9e8791de769d6751d0739ca719c6b,
+    0x7b7e5f77d5f37c5ef7b5eb7a5e778de177def075db7ac3f165fd1ec577e477155f51cc537c46f145ed13deb15e11ea46712de513e631845b1644975c49d4441a554f12c4582d452074310c811,
+    0x783d0f03b1be1c86c3f9767e2e6170ca3a1063b0a62791a459124310841106c,
+    0x1851b4550f4,
+    0x1b11cc,
+    0x7b4c56f57551525435,
+    0x1e8b82d8b22c0aa2809a240822,
+    0x7d0ec390cc2d2b4290aca70a4b13fd5bd940fa8593dbcf3547dd28cd30440dd34235274bc,
+    0x645815454354932429,
+    0x1ad6959d6156d535,
+    0x62af9bc6,
+    0x7fef7bbee7b7ed7b3ec7afeb7abe57e9e8795e3f81aed87e,
+    0x1fbbceebb8edbb4ecbbcbc3aeeb3aaea3a6e93a2e839ee4058e53b05630ce2bae5599c798c6e80dc3,
+    0x15f89ee583a,
+    0x7efebf8fd3f2f52d0b3bc8f1bfe7,
+    0x1d7ebf8fd5b27c1f,
+    0x44b,
+    0x7d0fffdfeff9fdff5fcfdbc5f31fbfedfafe9f9fe5f8fe1f7fdbffd59f57ff9fd11fcd0ffbd81e,
+    0x1fb3cceb36cd332cc32ecabeccab26c9322c831ec731ac5b14cc9d2c9be62432223b3c1d0cccbb6cda1fa1c8eadc0e8d89e4d8b6e3835edd39cdb0cac6b58da8e835b4c6534ed90de32b4461b5a358c0d,
+    0x47c,
+    0x12b02c,
+    0x798a71389723c7f19c5711c2f07c0f01c,
+    0x6498250d3344d,
+    0x7ddef79dd773dc77f3bf7d3b77b3af793a7773d4e7dccf1397799bce3d876d37f6b3775bda4d9d5f673df253966fc8cebc84d5d7cd3d4763c74cfd6f1b3671935cd535e0fc4ccbc44cf334c5c2cc931ccdd14c332f413,
+    0x1f27e52a385,
+    0x1c57fd765bd0f655,
+    0x1fabcaeab8afbaaa9aa2a6a96a4a90a2282a,
+    0x4d6,
+    0x7eee374dcb6eda35aa5a8ed4286d137e12304cf93c112fa1,
+    0x79ddf6bad773dc76fdb76bda767d9763d875fd7759d5f53d3f49d,
+    0x5cb6ad8bfbd4b19ccb2afaf,
+    0x1fefdbeef9bdef3bc6efbb6e9b66d7b4ecfb36cbb1ec5b,
+    0x1d2face336cd332cc32ecb320bab28c9b24c8b20c731aca818c5b280530cc98027,
+    0x7ffe71587e559ad91d3745dfcbdf,
+    0x1f87c1e8781d8741c8701b86a1e32819876c90621cb2ec806cc706ac6866ce2d818b20ccad61505ec485cc405ac3858c3056c6aca1530814b10b91c61431e5106073b1e7330ab69c2161d6741e02810e729c6c59067508472100c2084409c0e00402,
+    0x754cd2f4ecfbbe4f73e6f5395333d6f138d2f3d72fbb4eb3b6e9385273af29b94e33972137ce1c74db386d9354e3f7ed337fd1366cf36fcd367cb34d11f24cdf3505f14c7417014,
+    0x169164410c419004,
+    0x7f4f53b4f7394ef334e7314df2f4b535cad33ca52fc9d254af234851f4751b46517455134450f4350b42507436058,
+    0x7cdf2b8ddb7aad372de2b0dbb76ab368dd2a6dcaa4d8370a6b56dba92db2aaa92a0a7a9aa52ba2e0b62d0b02b8ac2a8a82989a588965789456892560905488c5408852884518805,
+    0x759ce719b669996a1a8f77cafb1cbf2dca727c8f19e7f1dc579576ed176f0fe6717c5709e4f05e3f0bc2703e1dc3c0781305c1c,
+    0x7e0817c0797a06178059740417203970021465b82c0a8280982402a620225e0015c0125a00a5805800950120,
+    0x1fd7d5ed795dd755cd715bd6b5a567595635855f5755b5765b966579565193e4b926459,
+    0x1f3baee3b6ed3b2ec3aeeb3a8e9ba2e7b9ce6b98e5b94e4b90e3b8ce2396641886,
+    0x71fbff1ab7ebfa7d1a269df5fd5f4fcff0e87ff4c3f0681f,
+    0x1f9bc3f1ba3e9b83d8f86d0f23d9b03b8f46b0ea3c9a83a2b0698e4a7aa43b9a2372a03f058ab19e3e05c5529c3c86a668ec1a1983a064658e4189943804c548e0670503685e638d61698c3485860948f28ce139c83498a141881120a61846310c861042300c66084260042d,
+    0x1fdbd6edb96ddb56cdbb1e4716d4731c46f6bc6d6b46b6ac696a46bac7a31b7a76af9f185a7e7461e6d9de645315f9115d95e3f8f1558be2c49e3585e2441e1d85105831,
+    0x1ebf4fc3ecfabe8f83def73d8f4bccf2bc8f13c4b0bc0f,
+    0x7dfeff9fdfffbd7f3ff6d379ee5b87d7b27cf7,
+    0x1f9fc7e9f67d1f27b9ea799f8fdbe47d3e07cbec4bbecf71e6f93da79120f73d67811af49d8f6114453ce043ce4300a433ca7280242bc6021c401bc2013c0003c07,
+    0x1fdfb7ddf37aeef7ade9b9de578ddf775d975dd37fc3fff4117e43dfdc330efcf79c23036e7f7417077d302f0d0478d92c097378900509f1c09517c501d4350641f0c011,
+    0x688f93c4923a4e1367d1f07b9dedb1ea7a1e4792e07f0783e8743e05c7c8f6159e86d0666b8f2189b0171966b86c3498aab04e6a8ea131a8129a610a866a0e41cb82698e2101a0188dc1,
+    0x777c5f38ade37,
+    0x1,
+    0x7f8fe7d9ee799d6719be6598e6197e5d9665594e5193e4d92e49916439e501c,
+    0x7e5,
+    0x1fdbd6edb96ddb56cdab6a5a768d9f6759b665976559363d8d675fd455d3745cf7ec3902df7025f101dc57b4037ac017a4270,
+    0x7e9f27a9e2769d2729c26698a5e9,
+    0x7f5de7d5ed739b66b9e56999e5b9,
+    0x1fa8861184e,
+    0x1febdaccf132dad39ce7b94e3374c76159b364d73,
+    0x7a6e1b66d1b26f8706f06e6e8781b1b61a9a66d0626c8606c06e169a8bb0566a862b49a8141b839870339a415aec3a0da188ea469caa78ceb60cc62854950fef40c46104c3,
+    0x6d6a5a768d9f6a69965d956645365c516545113c57e3d8d12d8b1,
+    0x7a2e0be7d8bc7d0a67c8b0289ee279ec261ea251e8298927908e731e228088778867709a209d825092238807308a2,
+    0x1fef37,
+    0x70bc9eaba1fe091fc07afa089f80d8207c81e7c02e061ea059e8041e60880a778087700474808010027,
+    0x1fdfd7edf97ddf57cdf17bded79de578de177ddd76dd9755d3785b3b6d8d615b75cd6d1bd4b70e836,
+    0x7e4f13a4f9744fbba5c12a5f3a25797ed717ea61545417ca397eb314a5217cf19741fb301096a101661,
+    0x7b4e51bc,
+    0x1f93c4c12c4a1244811c4610883108419024,
+    0x1df35c,
+    0x1,
+    0x1fd7d5ed795dd755cd7f8c56f5b56b5bcbfca5675956157d5d5f71b5657f05d7b055535cc115ac0f5940d52d610255f01d5b05c17b4429e154d005490,
+    0x1b96c5a968591605715a532465,
+    0x575,
+    0x4caa982a,
+    0x71e3f89e,
+    0x7e1f07a1e0761d0721c06e1b06a1a066190621805e17054d6874360561c0d21b0d01a8ce198cc14012738c63000c5,
+    0x1,
+    0x52f23c67,
+    0x7dfeff9fdff5fbfebfa7e1f7fc9f2dc5f,
+    0x1,
+    0x6508417087d30f4a5edc8f0ccaf22c1fe7489077914170921c83c4f91e2f8710c43e,
+    0x1db34ccb30cbb2c5b32aca326c9322c831ec733e36b246f0f836314bd8d89c8e6388d4c719a34b163430cb598ec50ccc40ce638cac1886c108410a02c,
+    0x1e737cd731cbf2dca727c8f1dc6715c4f0fc2f07c1703c460b807058,
+    0x1fb3cceb38c8b0cc0b204,
+    0x7fcf73bcdf35cc72fcaf3feefb9ed7b1e07314,
+    0x1f37ade376dcb6edb368d9362d835ed6b56d434cd2346d0b429,
+    0x7fdf77bde777dbf6bd9f65d8f61d7f5dd6f7f0f419decb925f772d4b3257712bca54b49f8a493d9ca5276232849987c978475d26c95894d72375322f512348361f4192c872,
+    0x7efd93cfebf8fdbfe5bbfa51b50473d4f4bccf,
+    0x7f5f57759d655855b55d4d506475,
+    0x11a84afb82a,
+    0x1febdaeeb9adeb5aceafab6a7a8e9fa5e91a2e83a,
+    0x1fbbce8a72cc32cc9a929931ec731ca5b16a3b3e35286cf0fa3,
+    0x65ed771db76bda767d9763d875fd4f63a,
+    0x7ebeaf6bc2dcb51faf,
+    0x1feff7,
+    0x76cd32eca326c831ac6314c4b0ac23120380a0,
+    0x1b729c9f23c7f1dce6dbcc6d9ca6d5c473f21f19af4b100f2d0a4270ec8fa943928c3725fc9ad49d01651fccaf25c0ff,
+)
+
+
+def unpack(number, bits):
+    values = []
+    while number > 1:
+        values.append(number & ((1 << bits) - 1))
+        number >>= bits
+    return values
+
+
+def kernel(aff, words, s_out, deg_out, table, block, mid, arrived, far_words, mask_rows, far_mask,
            col_sums, row_sums, row_shares, col_shares, near, far,
            load_sem, word_sem, leg_send, leg_recv, hop_send, final_sem,
            row_send, row_recv, col_send, col_recv, pair_sem, out_sem):
@@ -49,12 +306,8 @@
     def group(n):
         return pl.ds(pl.multiple_of(n * TILE, TILE), TILE)
 
-    def place(cx, cy):
-        return (cy * 4 + low * 2 + core) * SIDE + high * 4 + cx
-
-    def steps(n):
-        shift = 2 * (n % 16)
-        return (X_STEPS >> shift) & 3, (Y_STEPS >> shift) & 3
+    def place(cx, cy, cc):
+        return (cy * 4 + low * 2 + cc) * SIDE + high * 4 + cx
 
     def mirror(device):
         return (device % SIDE) * SIDE + device // SIDE
@@ -78,22 +331,40 @@
 
     to_partner(words, far_words, word_sem)
 
+    kind = (((high % 2) * 4 + (y + 4 - high) % 4) * 4 + x) * 4 + low * 2 + core
+    for outer in range(16):
+        @pl.when(kind // 8 == outer)
+        def _():
+            for inner in range(8):
+                @pl.when(kind % 8 == inner)
+                def _():
+                    sends = unpack(SENDS[outer * 8 + inner], 17)
+                    relays = unpack(RELAYS[outer * 8 + inner], 10)
+                    for n, value in enumerate(sends):
+                        table[n] = value
+                    table[CHUNKS] = len(relays)
+                    for n, value in enumerate(relays):
+                        table[CHUNKS + 1 + n] = value
+
+    relayed = table[CHUNKS]
+
     def leg(n, carry):
-        dx, dy = steps(n)
-        relay = place((x + dx) % 4, (y + dy) % 4)
-        direct = (n % 16 == 0) | (relay == partner)
-
-        @pl.when(direct)
+        entry = table[n]
+        relay = place(entry & 3, (y + ((entry >> 2) & 3)) % 4, (entry >> 4) & 1)
+        slot = (entry >> 5) & 127
+        number = entry >> 12
+
+        @pl.when(slot == DIRECT)
         def _():
             pltpu.make_async_remote_copy(
-                aff.at[rows(n)], arrived.at[rows(n)], leg_send.at[n], final_sem.at[n // 4],
+                aff.at[rows(number)], arrived.at[rows(number)], leg_send.at[n], final_sem.at[number // 4],
                 device_id=partner, device_id_type=LOGICAL,
             ).start()
 
-        @pl.when(jnp.logical_not(direct))
+        @pl.when(slot != DIRECT)
         def _():
             pltpu.make_async_remote_copy(
-                aff.at[rows(n)], mid.at[rows(n)], leg_send.at[n], leg_recv.at[n],
+                aff.at[rows(number)], mid.at[rows(slot)], leg_send.at[n], leg_recv.at[slot],
                 device_id=relay, device_id_type=LOGICAL,
             ).start()
 
@@ -104,21 +375,16 @@
         def _():
             lax.fori_loop(first, last, leg, 0)
 
-    def hop_of(n):
-        dx, dy = steps(n)
-        source = place((x + 4 - dx) % 4, (y + 4 - dy) % 4)
-        target = mirror(source)
-        return target, (n % 16 != 0) & (source != target) & (target != me)
-
     def hop(n, carry):
-        target, used = hop_of(n)
-
-        @pl.when(used)
-        def _():
+        @pl.when(n < relayed)
+        def _():
+            entry = table[CHUNKS + 1 + n]
+            source = place(entry & 3, (y + ((entry >> 2) & 3)) % 4, (entry >> 4) & 1)
+            number = entry >> 5
             wait(mid.at[rows(n)], leg_recv.at[n])
             pltpu.make_async_remote_copy(
-                mid.at[rows(n)], arrived.at[rows(n)], hop_send.at[n], final_sem.at[n // 4],
-                device_id=target, device_id_type=LOGICAL,
+                mid.at[rows(n)], arrived.at[rows(number)], hop_send.at[n], final_sem.at[number // 4],
+                device_id=mirror(source), device_id_type=LOGICAL,
             ).start()
 
         return carry
@@ -194,7 +460,7 @@
     near[0] = row_total
     near[1] = col_total
     to_partner(near, far, pair_sem)
-    lax.fori_loop(BEFORE_SUMS, CHUNKS, hop, 0)
+    lax.fori_loop(BEFORE_SUMS, MAX_RELAYED, hop, 0)
 
     wait(far_words, word_sem.at[1])
     for t in range(groups):
@@ -230,15 +496,13 @@
         wait(far, pair_sem.at[0])
 
     def hopped(n, carry):
-        _, used = hop_of(n)
-
-        @pl.when(used)
+        @pl.when(n < relayed)
         def _():
             wait(mid.at[rows(n)], hop_send.at[n])
 
         return carry
 
-    lax.fori_loop(0, CHUNKS, hopped, 0)
+    lax.fori_loop(0, MAX_RELAYED, hopped, 0)
 
     def share_out(n, carry):
         wait(row_shares.at[col], row_send.at[n])
@@ -269,8 +533,9 @@
         in_specs=[pl.BlockSpec(memory_space=pltpu.HBM), pl.BlockSpec(memory_space=pltpu.VMEM)],
         out_specs=(pl.BlockSpec(memory_space=pl.ANY), pl.BlockSpec(memory_space=pltpu.VMEM)),
         scratch_shapes=[
+            pltpu.SMEM((CHUNKS + 1 + MAX_RELAYED,), jnp.int32),
             pltpu.VMEM((size, size), jnp.float32),
-            pltpu.VMEM((size, size), jnp.float32),
+            pltpu.VMEM((MAX_RELAYED * size // CHUNKS, size), jnp.float32),
             pltpu.VMEM((size, size), jnp.float32),
             pltpu.VMEM(words.shape, jnp.int32),
             pltpu.VMEM((groups, size), jnp.float32),
@@ -281,10 +546,10 @@
             pltpu.VMEM((2, 1, size), jnp.float32),
             pltpu.VMEM((2, 1, size), jnp.float32),
             dma((groups,)), dma((2,)),
-            dma((CHUNKS,)), dma((CHUNKS,)), dma((CHUNKS,)), dma((groups,)),
+            dma((CHUNKS,)), dma((MAX_RELAYED,)), dma((MAX_RELAYED,)), dma((groups,)),
             dma((SIDE - 1,)), dma((SIDE,)), dma((SIDE - 1,)), dma((SIDE,)), dma((2,)), dma((groups,)),
         ],
-        compiler_params=pltpu.CompilerParams(has_side_effects=True, vmem_limit_bytes=24 << 20),
+        compiler_params=pltpu.CompilerParams(has_side_effects=True, vmem_limit_bytes=47 << 20),
         name="exchange",
     )(affinity, words)
     total = size * SIDE

time: 166 us -> 184 us (1.11)
  the two profiles are of different devices: /device:TPU:185 before, /device:TPU:9 now
where the time goes in v3:
time: 184 us
  Pallas kernels  179 us (97%)
  other arithmetic  3.02 us (2%)
    pallas_call x1, Pallas kernels, on_device(): pl.pallas_call(kernel, out_shape=(jax.ShapeDtypeStruct((size, size), jnp....  179 us

profile of v3, /device:TPU:9, one launch (start us, length us, event | category | flops | bytes accessed | tf_op | source)
XLA Modules:
  0.0 183.9 jit_solution(17791884733307745336)
XLA Ops:
  0.6 0.0 copy-start
  0.6 0.7 copy-done
  1.4 179.4 %exchange.1 = (f32[1024,1024]{1,0:T(8,128)S(1)}, f32[2,1024]{1,0:T(2,128)S(1)}) custom-call(f32[1024,1024]{1,0:T(8,128)} %aff.1, s32[5,1024]{1,0:T(8,128)S(1)} %bitcast.4), custom_call_target="tpu_custom_call" | custom-call | tf_op jit(solution)/shard_map/exchange/pallas_call | solution.py:527
  180.8 0.6 slice_multiply_fusion
  181.4 2.4 %multiply_multiply_fusion = f32[1024,1024]{1,0:T(8,128)} fusion(f32[1024,1024]{1,0:T(8,128)S(1)} %get-tuple-element.4, f32[1024]{0:T(1024)S(1)} %bitcast.5, f32[1024]{0:T(1024)S(1)} %bitcast.6), kind=kLoop, calls=%fused_computation | loop fusion | flops 2097152 | bytes 8396800 | tf_op jit(solution)/shard_map/mul | solution.py:557
Async XLA Ops:
  0.6 0.8 copy-start

commit v4 on v3

--- a/solution.py
+++ b/solution.py
@@ -10,8 +10,6 @@
 TILE = 128
 SIDE = 16
 CHUNKS = 32
-FIRST = 8
-BEFORE_SUMS = 12
 LOGICAL = pl.DeviceIdType.LOGICAL
 DIRECT = 127
 MAX_RELAYED = 114
@@ -389,7 +387,7 @@
 
         return carry
 
-    legs(0, FIRST)
+    legs(0, CHUNKS)
 
     def start_load(n, carry):
         load(n).start()
@@ -442,8 +440,7 @@
         return carry
 
     lax.fori_loop(0, SIDE - 1, share, 0)
-    legs(FIRST, CHUNKS)
-    lax.fori_loop(0, BEFORE_SUMS, hop, 0)
+    lax.fori_loop(0, MAX_RELAYED, hop, 0)
 
     def share_in(n, carry):
         other = (col + 1 + n) % SIDE
@@ -460,7 +457,6 @@
     near[0] = row_total
     near[1] = col_total
     to_partner(near, far, pair_sem)
-    lax.fori_loop(BEFORE_SUMS, MAX_RELAYED, hop, 0)
 
     wait(far_words, word_sem.at[1])
     for t in range(groups):

time: 184 us -> 145 us (0.79)
  the two profiles are of different devices: /device:TPU:9 before, /device:TPU:42 now
where the time goes in v4:
time: 145 us
  Pallas kernels  141 us (97%)
  other arithmetic  3.02 us (2%)
    pallas_call x1, Pallas kernels, on_device(): pl.pallas_call(kernel, out_shape=(jax.ShapeDtypeStruct((size, size), jnp....  141 us

profile of v4, /device:TPU:42, one launch (start us, length us, event | category | flops | bytes accessed | tf_op | source)
XLA Modules:
  0.0 145.2 jit_solution(7993247531212811361)
XLA Ops:
  0.6 0.0 copy-start
  0.6 0.7 copy-done
  1.4 140.8 %exchange.1 = (f32[1024,1024]{1,0:T(8,128)S(1)}, f32[2,1024]{1,0:T(2,128)S(1)}) custom-call(f32[1024,1024]{1,0:T(8,128)} %aff.1, s32[5,1024]{1,0:T(8,128)S(1)} %bitcast.4), custom_call_target="tpu_custom_call" | custom-call | tf_op jit(solution)/shard_map/exchange/pallas_call | solution.py:523
  142.2 0.6 slice_multiply_fusion
  142.8 2.4 %multiply_multiply_fusion = f32[1024,1024]{1,0:T(8,128)} fusion(f32[1024,1024]{1,0:T(8,128)S(1)} %get-tuple-element.4, f32[1024]{0:T(1024)S(1)} %bitcast.5, f32[1024]{0:T(1024)S(1)} %bitcast.6), kind=kLoop, calls=%fused_computation | loop fusion | flops 2097152 | bytes 8396800 | tf_op jit(solution)/shard_map/mul | solution.py:553
Async XLA Ops:
  0.6 0.8 copy-start

commit v5 on v2

--- a/solution.py
+++ b/solution.py
@@ -10,25 +10,280 @@
 TILE = 128
 SIDE = 16
 CHUNKS = 32
-FIRST = 8
-BEFORE_SUMS = 12
 LOGICAL = pl.DeviceIdType.LOGICAL
-OFFSETS = (
-    (0, 0), (1, 0), (0, 1), (3, 0), (0, 3), (1, 1), (3, 3), (1, 3),
-    (3, 1), (2, 0), (0, 2), (2, 1), (1, 2), (2, 3), (3, 2), (2, 2),
+DIRECT = 127
+MAX_RELAYED = 71
+SENDS = (
+    0x1fff07bf83bfc1cfe0dff06bf833fc18fe0bff05bf82bfc14fe09ff04bf823fc10fe07ff03bf81bfc0cfe05ff02bf813fc08fe03ff01bf80bfc04fe01ff00bf803fc00fe0,
+    0x1fff014073dfc1dfe0e7f06ff835fc19fe0c7f05ff82dfc14fe09ff054ad65fc11fe087f03ff81dfc0d5f167f02ff815fc09fe047f01ff80dfc04fe01ff00bf803fc00fe0,
+    0x1e189a7f80c0e942a1f998c8907c5e240c4b95980093a56311e1d928c068542acf181d0c8b080e6366e121c8b8b438701a271434069ac28441243082b0188418ea0225001,
+    0x15951fff8041c97373f7f077f812507cfe0dff050b4f5fc12273cff063f82dfc0301430e1bc74ebfc0c1739ff047f821fc0efe06ff0143cd5fc08fe000021ff8021064fe0,
+    0x1f7f077f839fc1b780d7f065d031fc17700b7f055b00403b46809ff049783e93915a087f03d48080eae4c06ff030f00002ab32057f024a011fc071e037f0144807fc01020,
+    0x1fff07bf83bfc1cfe0dff06bf833fc18fe0bff05bf82bfc14fe09ff04bf823fc10fe07ff03bf81bfc0cfe05ff02bf813fc08fe03ff01bf80bfc04fe01ff00bf803fc00fe0,
+    0x1482cdda0bcce55622eb1950a99a0bb2246e2f913f836ba53522d2894510b2964f422c22938e8ac824c34281b90c0a44032b282f88f1c70944a41fe0405b18408a1640022,
+    0x1703477f830097b392e7f06bf833fc17fe099515bf81a3c552b2f016d3f80c187121228527c1421fc0b1527ff024448814e70f267f0480742006afe00013a3f8040043fe0,
+    0x1a06b653876ae29fe0f8c9d878eeaa351a3984b45184dfc0f42127f03858fc226c103901b34f87a1e6a0a30ff02ce06086230ecd049a0a0700e6206c29389c10f81280040,
+    0x158957ff80a4d3efe050a377f839fc1bfe00807543db5fc19fe0c7f03846affc130b6b7f053f825fc11fe030c0c3f80610cffe06ff033f813fc08fe000031ff809fc02fe0,
+    0x1fff07bf83bfc1cfe0dff06bf833fc18fe0bff05bf82bfc14fe09ff04bf823fc10fe07ff03bf81bfc0cfe05ff02bf813fc08fe03ff01bf80bfc04fe01ff00bf803fc00fe0,
+    0x1fff07bf83bfc1cfe0dff06bf833fc17fe0b7f06135c20154fe09ff04bf823fc0ffe077f037f819fc0bfe057f027f811fc07fe037f017f809fc03fe017f0405fea78e0fe0,
+    0x14ff07841fe7f965402ff0301afa96144e0e2284d20348612400c1e8447b36538f340b90e38b020520a2006908080bd63e081c0a88b8c12ce2a0414030886401c20e000c0,
+    0x1d9e098241009f9157c1a0fd1474593e4119950dcd4644436137e863d4ac7810f40f780e0bc8c5a282b1d15070b02ed218230303840b80dca0c240f18ff00824420020031,
+    0x1f7f02511fbfc1c742d7f065c0b657d86c2f8ed5d98adfc15602a7f04d68a5fc1154287f03d3884276e4626ff030f097fc0a30247f00403cffc062422ff0106087fc00042,
+    0x1fff07bf83bfc1cfe0dff06bf833fc18fe0bff05bf82bfc14fe09ff04bf823fc10fe07ff03bf81bfc0cfe05ff02bf813fc08fe03ff01bf80bfc04fe01ff00bf803fc00fe0,
+    0x1f7f0189218779dfe0e7f06ff835fc19fe0b7f057f829fc180449ff04bf823fc10fe07ff03bf81bfc0bfe0f82a2bf82e028018c4ff023f80ffc05fe027f00ff805fc01fe0,
+    0x1bff05bf82bfc1347cd8f0f86469fc12fe08ff03bf81bfc0b2fc00067c0d32302afe02074c007de1029fe06010a3f80ffc06fe02ff0703447fc1d03e17f0600c43fc1a015,
+    0x1797f17f805fc110c6e0696093183bd506250cf5c8b1027d61ecf8ee1c3bbc37941acd8291033ba2b9316cd08e404b32068e10c081f2c3b2407290ac685e18230003c300c,
+    0x160f5fc5e32598a47f806478d4ee559d21cb14607f81c1518014a1362487e4419c1fc68e66c672624fa17c58c6544f0c298f0fc20342107c619870dc8971942704098001c,
+    0x1f18cdd0b3473953ace16cd0db3267922ecd9eec7f826578d24cc1beac8b1c4b8ffe0b17ea3f82053aa16d60ce184b522f8716c286e0ff83e17e210c208e802b3a020102d,
+    0x15052f58f4e10b5fe08ff043f81bfc1f45967f0717772a1be3d9ba56a3f82891ba51d9206e12f4dfc1649d7196eca647fc133bd5926bcc74a35a91fd2054884f4208a005d,
+    0x1784ad880960eb51e26adf30cb7e5e41fe0f15928bb7a52492cde1391d03b64a4828dc16ecc58b43e5214230cd14836847b00e288ee905b72264310d708e88236e224002d,
+    0x168d5fcb4e658721da58c5d04f62507e2538131bc275c407d21360e1a8ef8a217c1d348b1ec5cd059da1533891841f4820791133107603cc415d70b31841d814c00075013,
+    0x1508c543a8c1702fe08869c832be1e0f0aa6049b42283fc0b06ae88d2023b8175e1c1d84d241281fc18161d03d1c0aac0b43048701d5c504a0a74121200d4c40720a100e1,
+    0x1fff077f839fc1e136d7f06c35aa20d9fe0c7f04ff8281cd1fe080633ff81614d709667f027f811fc160763ff048159c2ca4fe050430bf80c0ccd03628130c058200c0fe0,
+    0x1b92d44429dfc05fe07aaf6479989bcb0aaf8fb0bf83c36c738e0ff06071942f561a6000dd061ba32d3166305d4851b82ed0126d8ab1053b426cd0e6a87b24219012c3046,
+    0x1ebf778c6b6f5d70b6cbc77dcf840c7c71ec3b769bf8208766de6ff0140daae5d46be9b770005e2d5d269e7b27419798bdce61e52b72d4f9095c949e39b718cf8835c31be,
+    0x1f8dbf441ea32fcfe0dff06bf833fc18fe0bff03832edfc14fe0f06dc831e7fc10fe0604dbff8100f710a75ff03421ce1ae400b283babf813fc06fe017f007f80606e0fe0,
+    0x1a073f05df0357915730c2d84dea316f199b957c445e42d6a09780a58815dc25600172082e81c1a217d11b4875ec3ed80c3f0f14055cc2ece117e09108269416d6002301b,
+    0x1fb5fd8bafcd3fc62fb91ded7bc80af95afeb3fd563c40b5456f88ddcd3bf4c3f04afc2dfbd1be4a7ed42f728fb103d69bea32f41df9c9bcc4be516f483d8c3bc20be004f,
+    0x191d7d117fa3cf039fe0e3cc2ef434ff117c8c3b426f02cfe0f740c79047ec28e307f4ff06c35ea20e5fe08873dc2ddc18ef0976053880fc005e1fe05033ac1dcc00e7037,
+    0x1ea6a27f83e4b984043ff05cf928bf163c4f11e54e924b713384c81e44d90dfc1034427f00ff805fc0f3240ff034c138968e64807f02cb9368e8a2c4d22a2099183e85144,
+    0x190c77c6476643e171a9524cc61c2ddd355c170c4651a54bc2f5b950c03c9425da25548875885504421fe038c2acb64a20af1552070b03d6815a3095103083f80c09d901e,
+    0x1f8bf2428bc42e408ce8fbecb1ce12c206ce0ebe8a1f232f6267514d5491f02ae5006604a5089cc3f52207b89bc471e622e312a807bb459de1aeb127083d2039ddfc000c7,
+    0x17842785517fc1a134d953840f3aa17f5dbca45f166ec89774fba9c5e0451208944bb20124c3d0009920d489a594165c616d3fb6165a8cec4008829b30f5c02d061567014,
+    0x1f1ea34897a7685fe01ff07c68366a8b1a5c98a4489305a80fe0b15a3c69101aae184a11a0801742fea16498da703be42e89124809a542bd81e870a4304a10092e0b61004,
+    0x19a42e7f82dfc15fe09232fc5f6288b4fe07a129bf81c80be6d969f2f1a65874a5fe01ff06996566cb76190ff075055464bb3b54972e0dd5048a0fe038f2c04d4808a2055,
+    0x1e16b34c27e77381c6f1bcdc61ba6b35166d98cc851b453335cac93cbd62840a861c98abd2c296c3f2c50aa0dc8c525c1f2a48a4a3d04326036c732a409b10118a2f40049,
+    0x1f1133bf83840c319b6842fcbd8814e5057d0f3080df034dd2965832802ecc19fb2763822d80fc200b923698932bf8241cd72168863547d9e10d41566033403d9204c8076,
+    0x1f898e7f83a22300ecf07b4c40364e8b0cea0ce3c33222f8e0ac48ae301810278608c686a141b381e38241bff010132bfc0302cd048d878440b0a141005e1c30640621021,
+    0x1b9a6f46c6a65a40549986e8b7625db929d7966e09f5c55b425d6146b48f544dbc151d980a4875049a71ddf8777835a015c61bd2906dbf824402315d589088474209a005d,
+    0x177f033f83e8fcafe0f22f1ff80dfc1c38eea1f64dbb483d832eb9ef58bbaa73d428e1ff0488ba667c2fe0816f6df2a25b4f1ae691f2c4b9237c0fe0407f14238807c100e,
+    0x1c4054ff83469dc77a8ff07cff9ffc0cfe0c98774efac59d737ea93750d793fc1231e80e76dd69c31cd21e2ff02c779421de0d640570ff805fc0709e0800981f81fc0401e,
+    0x15ff065ea30c703fe0f0f86c832c5b941eca95e1419e453810cb893e34733a3a0c1ace0c85c801e438918cfa1a1c5b1c3f931c050ee40580c3788120001b904b34220210c,
+    0x1b897f8345c45bd17ab115d45ee80df213b88c5f0569e195b13a6895fc2fc809f811a5104cc1ff238300ba5835302692117a05140250407ce054607a180508168a056001a,
+    0x1d0293ff83e97f84af5ff0551bfc8bf442fe81a27f83883e7fe0d9efc8ebf273f036fb19fb8cbe65fe5fe0894fb0abc7fc02fe0b80907f801fc0824f691f986bd437e40ef,
+    0x1da97e80daea1f8fe0aa77a7f82899ff49f9247f91fec10fd43f7a07f0ffda7df93bf61c7ccdfd469f031f4187b8afe204eb27f31178bf8083de71ff0ff01467c1fc0313f,
+    0x1f0ae3c7b33fc16fe0d09e53f827fc0c0ecfb2a243321fc1d7c4e30a1c2336ba8efe0504e61c9080f8bfe0baba23f80dfc0102caaaa45610bfc03fe0924a0bf81a6e80fe0,
+    0x1ebb2796530291f0fc998297f836dc943f58962c8e574c49c0dc8132bccd5c3cac255cab22c855220a8155b85634460e14aa0d820040c356c94820b53006041d6a5480015,
+    0x1d21bf0620c0335168a05a90127a0e922e7c9ebb4190bfc03029c1abc4522c5efb143f88c3c91c3fc0a227f07c2469c1fc0b024986c384a202ae2009605c20420e0b17043,
+    0x1f7f024260c317dfe0202673f837fc1afe0cff063f82ffc16fe0aff07c0d29fc13fe097f047f82005effe077f037f819fc0209b5ff02bf811fc07fe02ff00ff803fc00fe0,
+    0x1509cf1a929fc1b664f0de698125fc0ffe0ca9a61712ea29d280b26a55413e46f346477f0411122828bfe0105cb4f9184e88fe048ea18690e1e85fe0200a002107fc01fe0,
+    0x1f146aff832b0bb6f54ff069ad6cacbf0bdaaa29ff81a35385b5a292dd657835a5fe09262cd4d6088b14f507f03d355c74bd07d61b2a11d4c5ca41b550648c654401a1175,
+    0x1eff0502279fc1bfe0cff063f82ffc16fe0aff04ff823fc1210e6ff0402b5433460ca5ff024897e23c5fe0793b0ff80e46ce06ed0aab0237c0242fe00ff0201b41fc04069,
+    0x1d856608dfc11ecfe09046701f17fc0f13740a5e44f4e20e609728165847542cc90d6f8649017060cc2017b85483f802019d395a932e8856819b30fd8032c4375c09ad0bd,
+    0x1303d6cd1f42f95327207b7813be8213307727a44b9fa6e102c7e1984853305e17200b0fbb499e83aec24778dbac81d42ae81c7c87f9c51d217850e7186b8419c406e0007,
+    0x189a6e82f980d5f2f691230416a044de2d67903087e5c3cdd2b668e370a59634db276001564959430d823648b35c859028d61f6389354758a20d41b620734c658614c60d6,
+    0x1f0387ff81c62c5266eff073f837fc1afe0cff00412b1fc17fe0b7f057f829fc13fe097f047f821fc0ffe06ff033f817fc0afe04ff023f80ffc06fe027f00ff805fc00fe0,
+    0x1eff06d65b9fc1afe08a6363f82dfc15fe097f043f81ffc194f6f031fc3799fc0007b69f35d0d97fc143f647f0080f5405d33d63ff038d5925cc6fe027f00ff80a44c1fe0,
+    0x1f9c870631dfc1d1c099fa2bf82c4a1238481aa3cc1283a1b02f696a2c99222a152873ff0684012468102b40da60300a2697080185a13f8180e020e430186403fc42e0064,
+    0x1c1e0b19d6c703f431a1a0f8fc64603d3918160f0cc5c503b2b16930e89c56403923150e0dc7c522c351d140a0cc6c4c24311712860bc444810270b110308c1c420420031,
+    0x1e7f06ff835fc18fe0b7f053f825fc19607e83f43f81ffc175c777f037f83ecaebfe057f05551ca1b69fe047f04d31fcaee302a082b44f9cffc0c36737f013f8003ee2fe0,
+    0x1f7f07d8ddea4fcfe0dff0757df5fc18fe0b7f057f829fc13fe097f047f821fc1955777f033f817fc0afe069e3a7f811fc174973ff01bf80bfc04fe000938ff805fc01fe0,
+    0x1fff07bf83bfc1cfe0dff06bf833fc18fe0bff05bf82bfc14fe09ff04bf823fc10fe07ff03bf81bfc0cfe05ff02bf813fc08fe03ff01bf80bfc04fe01ff00bf803fc00fe0,
+    0x1fff077f839fc1afe0cff078b66ffc16fe0aff04ff825fc11fe087f03ff830592efe06ff033f817fc142dd57f027f811fc07fe037f017f809fc03fe017f06c4643fc00fe0,
+    0x1e10f7c43b06a3e241a968f4806e23db1c1d09ee460664e36101686ed0304e17a514388f8c8205c2e230e32089881216222908d5068c0105016210633028bc08400a6c001,
+    0x18981d8dcf00d9ffe0f7f077f81c5c742f3e7f04cb4d84c7bfe0d7f040a4f3fc0f27350d1b48cce24691739006dff82bfc050f35ff0183d11fc000741ff01034c5fc01033,
+    0x1fff07a003bfc1c7e0dff069e833fc18760bff059d029fc1372097f045c02a7b8f6e081ca39a8022bad66067f02d6015fc094e047f01d200dfc053e027f00c7005fc00020,
+    0x1fff07bf83bfc1cfe0dff06bf833fc18fe0bff05bf82bfc14fe09ff04bf823fc10fe07ff03bf81bfc0cfe05ff02bf813fc08fe03ff01bf80bfc04fe01ff00bf803fc00fe0,
+    0x1dff067f82ffc1d662faa957f83c9e58562e2195120ac725a0ed919930c09c4e53fe08ff024a8880fa824287f018708a1a4ffe0104904209bfc0bfe057f00ff80e1320002,
+    0x1cb917c5f70e05e5d2bb61716c96113b15dab01694ca6b856492827144fc9a7c4f352e886b0b4925c4001357f0383f6819a81d290569c6c8a3c4605d20910c2c841441012,
+    0x1d1482012a2338402af188f0d04203db321a92864c05c2797261e948b04b304a34201b0e8b4302432331c1306e0c01a02a250607898ac48541e3f084000824304e1622061,
+    0x1fff07bf83bfc1cfe0dff0083775fc19fe0c7f05ff82dfc15fe0a7f00c07e7fc12fe08ff043f81ffc0efe06ff033f817fc0afe04ff023f80ffc06fe02ff013f803fc00fe0,
+    0x1fff07bf83bfc1cfe0dff06bf833fc18fe0bff05bf82bfc14fe09ff04bf823fc10fe07ff03bf81bfc0cfe05ff02bf813fc08fe03ff01bf80bfc04fe01ff00bf803fc00fe0,
+    0x1f9d3f7f839fc1bfe0d7f063f82ffc16fe0aff053f827fc12fe0c895c7f80828d0fe07ff03bf81bfc0cfe05ff07895d5fc09fe047f01ff80dfc05fe01ff00bf803fc00fe0,
+    0x1fff07bf83bfc1cfe0dff06bf833fc18fe0bff05bf81807e00e0aff053f827fc12fe08ff043f81ffc0efe06ff02ff8041b0afe04ff023f80ffc06fe02ff013f807fc01fe0,
+    0x117f06c148609f537cf300683678ac01fe0ca807d842e941d5900000e14c2688164f089e0511c1e70124507180410418580d370595028c4124c0823038f0187c082405070,
+    0x1f7f07628b9fc1b862d7f065f8b1fc177a2b7f055b8a9fc1362297f04568a1fc0f52277f0352899fc0b3a257f024d891fc072c237f0148089fc0318217f0043081fc1f086,
+    0x1fff07bf83bfc1cfe0dff06bf833fc18fe0bff05bf82bfc14fe09ff04bf823fc10fe07ff03bf81bfc0cfe05ff02bf813fc08fe03ff01bf80bfc04fe01ff00bf803fc00fe0,
+    0x1fff07bf82a067cfe0182c6ff833fc1d5ecc7f0691b2ffc1236cb7f03463160274fe09ff047f821fc0ffe077f033f815fc0004c4ff023f80ffc06fe0080c17f809fc02fe0,
+    0x1c122b83e27fc12399b902c09654111c175fb463ff8082129fe0f3160ff836a98b1b9283420666c1c350748850f437b481992fc6820d03f0e0422fe0300087f8180180014,
+    0x1f9d9b4433c6e6c0ece9a9c543ec1b860ace179c090f65a6f4afa01a3878f44e7228bc909ac60c7fc0a3ef983e041b30326938fb8b99c48d067e524fa879800b0443e4083,
+    0x1b966243dca14fd17cb1461056ea498ffe0a106040624399f07488d61c35e0318dfe070b6705718299b13c509678150021fa11c1802643f1019980bc30464c1704098b01c,
+    0x1103ca7f81847bc16b37f02c6b6a878a14dc9587c80304a0d188408ef8682e3e0e20cb0d814436832110cb206ef440261e070ac90580ff81e169b0608008042b400bba000,
+    0x1fff07bf83bfc1cfe0dff06bf833fc18fe0bff05bf82bfc14fe09ff0001665fc11fe087f03ff81dfc0dfe067f02ff815fc09fe047f01ff80dfc05fe027f00ff805fc01fe0,
+    0x1f21ea193b483bc462f9d92c498e9bdb3a22a5f64e0ac7fb7362a8dd30a36673b4302899ec8b8a063a20c6e9993898b04e4a0aa4899108b5e57a016d683d0c308c37a1002,
+    0x1b9511bf82c65bf47da986904fe65dbe45d9166f4aca255bb23270d170f75a2c5a3bd2867a03c941c5937d7936e0bf583db403310478027d635a107b4856c0574e0443019,
+    0x1f8cf50a8fa466602a204d0802bc23d3283083d4898f64270223e01f3c78f43a6e1a307f03060f2326b143c0a9a840ee22690e3b059a028ea126708388399418da0a63003,
+    0x1d7f07c6eb3fc15fe0a7f07866a5fc11fe0d8853ff8301d4cfe05ff0745eac1948fe098555c0d8ffc1c15a804517f81a0d4e0fa4825282e8c0cc2fe007f010058605c103a,
+    0x1f96d7a33b8dbc8fe0db5f6a23b2d3d882ebb3f4c52ba47567ceab1f51d3a4c3d168e828f3d639c0b4d46e2ff02d13986fca34e495f1c8b8c1fc40ee1ff007f8040bc002e,
+    0x1f4277c5ebb01dc65edbc74c55f4edd85fe7873dd67acbdd547e6063d10796397909392171836c3fc0e09781c744bf881d650376937285f92054813e38b70c0f8009c2017,
+    0x1c1486c52ca1bf712b99ce3419ec461510b915e03f8182f1022c713e7c58282e0a16c58ee1c4310338f0eb084c7828380b6908b189e101ac4139d08f883868100c0af9020,
+    0x18146abf80ffc19172611693f83418f81329053b47f5e10f711240417c3dd22dbd0d73031702de215760b25823d4248a04f4072f037ec25dc102207d07f04c0c8600e103d,
+    0x1fb1ff9d3c7fc1d70fe2ffedb3f2b7f76afb2afe8888e47d5202a29fc963f03e531c28a7fc133da87ee18278893103d01a41fe0283924dbc1fc0a04259af988bc8024218f,
+    0x1f397fd87faddfc5dfdb47d7f834c9f4fe097f047f82ec5eefe0b2e7b3f826a9e9fe0c1a5c127de89ed3ff3ff06496d675ea31f2003a0afcdfc03fe017f0146fc3fc00fe0,
+    0x12ff075293e8b99484f21e6119348a97444e20e5909367f943e41ff04cf12a829138491da40d11e6a80fe0698a38b9165a8c284494a2889103e871a430aa1041041681024,
+    0x178b0f86c7a809c434d1d26cfd1431bf0dda1b258e5246493334818244bd18588e2b46850ac9d12102725440f214750c2c8111518a2642c44189809100025c1c480035031,
+    0x1f93b3c60b84adb147d0fb64c1f032d52c7b0ab5c313c42ec0c6a07b48a9ce4b4d24798ebac21ba37c60a4805b2889dc2fc214a88dba479c006480662ff010018622e1024,
+    0x167f06084fa80f51f3d010940e367cf41d3c9e3c86cee70ff277b1b39bf820286f1938993f0151c5cfe23717f0345cc001131f73881ac4cc2008a1132103a05dd201830f7,
+    0x1fa6ae9097abf393e597f03ff83c96b638540ac3bf83892b5325da2ab3f8307ea9fe058484ca96e76b0205a17ab4bb4ffc0a1a5890a943949fc0308517f004094c0a00fe0,
+    0x1f232e7f83a80b5fe0c1e2cbf815fc010563ff01416e874a2fe099b283f82268bc6198182fd0d5c5cb73d5db148c0e34c12f35558f2b4a55230ac1f54062985d6c09240b5,
+    0x1a11cf0a8adfc06fe0503e8c0bfa325e145d8b968a0be56d9262889cdc90b02a55222208ac080a6264f1e2587cb870a41a4c142685924389013270a2101c9420821240042,
+    0x138e5e02fc82ced0b370a6d817f434d529960a4fca59625332594837941cd41d31219c8c340666e2cc3053a0937875a41cdd1360015f0359011bb0961034981e5e08c1019,
+    0x1482f796a66439d569fabcb06317fc0202e88ee28531e2b9b529e29ce5325a27974a9d25ca04b308f36469a9ec983b2477230cc386e510a4813903c9088b38b2400b85fe0,
+    0x1f186f096babd3f2b170c56c8694254615ec222903fb459b717dc974d44f6855a30de9936d85e8409c71369126c06f5e45b10fa6906b047563da009a48e684079035a509d,
+    0x1f98f694ba3fc1954ef17b61439dfc164ee57f01ff83a62d76aa37f0513389fc134aedabd0ff80a06b044e17f03d0381fc0d3ce922d2cd3b873c92cea96f20939817c10ae,
+    0x1ba4758c7f21c89190a21707f81e4cf023f91f7205c26a94e1bf8a857c1d1a65db19730879c47ca107d37e2031f0d7b0108307f1027f80d1851da19e50872c17aa088001f,
+    0x1e1ee3893f277982ecf0ffe809fedf0b20fb9be2873e037e616f68bf84107ad31428ca99e144bf6bb1126c409fd801c61fec4287a5c0833c8176004f996e1cca244f891cc,
+    0x1e156403f6e217e11b71c4c437d6157f6b860b6ecd71429a80bdcae41c1f70a51d5b83096e9560a21a405da9265936284589fe0997448ce0619a203d7944341ec00da103b,
+    0x1f0fac8cbf83ab12efb1ff83f83e224f28fd8797468a873f9162999fb08bf436b7102815fe0595c32b5125594f2473c643441ee68ffa05bcc2be50af084aa819441be7045,
+    0x1dff04ff80c74f50b7e1c7fd96c60dcdfe0c1b7f966ee69e9fe02ff0755eec59e4fe09157e946c5fc140578137e536dc41e1fe007f044a7d635ef1df6195a84fd019e71fb,
+    0x1fbba485b09fc187c4688e59e107fc1a348f3aa5cca0e0622fe0eb9a50c238e2912c8db6a41b132ce8e644ab2a2d6926c68a12c7afa03f818a2883a431fa242b0a3681084,
+    0x1f8a6791c53fc1d411c8761ff836989a318a9a270f53090b711427f0510d6c88b239599f2c0cd626caf2f517f038ad5a54a50d46122ac85543ca817530728c254204a0015,
+    0x1d7f074333e379c0acc7f03428fc2b9b08cbff024792dfc1906ca7f04bf82a27860438ff043f81ffc0efe0988e33f80e1f8bfe0284e2bf811fc03fe0100f1000c20380fe0,
+    0x1a15268371c4c9d13398c1a42f1a09fffe0511273f8060599fe0c7f05ff82dfc111d7aff04bf821fc0bfe047f017f80e05e4fe07891f825182061fe0304183f804047b013,
+    0x1faeae5716c3337585e2dae87336b2b5545c2aad141642b314e5f0be3ca27a2b8e1ac5aba286326a2a910c827aa0330e1f8608c6a4a901b1882a304c29aa880b02078000c,
+    0x1d956fca77251be27d47f074976e4dbc23da116e887663db64d588e6e07f6035b51dd78c6c8fd5a29ae3756096ac675421a915d3876984f4a19a40fd183688174205a001d,
+    0x1a06ec83357fc1e06e885ef05a7e233a129804d27f80ffc1810937f017f83a1f350c91ff03c2b45fc0e06dc85ca8136e3ab30a9b01cec0b9a0fa1066601ea00a41fc0400d,
+    0x1b074c4176a291d0d917f0200768251b09990847c5e1a1d1e1585064704e1c54f705948546846183cf90d83044602e200d2b09828341c16080903018782483f8020513019,
+    0x1388c18101a061dfe0e7f058a1860335266f15b5091b5fc13226f8cd28039dfc12206105a447997fc101c6002a23f83652c4fe0081c3c69b24ec90aac11b3059ae3ec50a6,
+    0x1c160d9156e503e371a930fc6da6483d3318910f0c46480bb2b178e0e89c5474b923168b098b55628341d14890909d4e14231b52830c04c44082e0f10042b024420028011,
+    0x1e83f1c08400704009fff05803bdfc011a6e7f06ff835fc19fe0c7f05ff82bfc14fe09ff04bf823fc10fe07ff03bf81bfc0cfe05ff02bf813fc08fe037f017f805fc0312a,
+    0x1b26360f5b7fc173b690d1ebf82a80d125740b3a465e078df2facff053f81ffc13316699338a599fc1d0935861f8968ffc02fe0514318658a0c641161883700cc00161076,
+    0x1b7f05c71e027992a07ff05469e65f182606a4a50903e46121870ff030803c420e167181fa4703a360b1e8e0882051f62ee70e088ab98281426e40e7284b8009f40e0202b,
+    0x1b0a364ed3024fd1d69883781fe01cd5354706344b51e489f0d250436c3dcc30ac01f403334852418fc15648d2684d9608f70b638a2501d8800e5174182304058000c2017,
+    0x140fb7999e2435a30b0ff06d81da3b595e728ab5d69fa7b7556758ad4d49fe96f24e7e23bc121e88aef427502f30f1dc76e914bc01918b1ce0744207b0090c29c416e0007,
+    0x1f7f077f82e8cfcfe0d7f07d05f3fc1b3d781a3e3f82dfc15fe09ff050e5e5fc11fe07ff03bf81bfc0cfe05943abf8121d661571023a3f80ffc010772ff013f807fc00fe0,
 )
-
-
-def packed(values):
-    word = sum(v << (2 * n) for n, v in enumerate(values))
-    return word - (1 << 32) if word >= 1 << 31 else word
-
-
-X_STEPS = packed([o[0] for o in OFFSETS])
-Y_STEPS = packed([o[1] for o in OFFSETS])
-
-
-def kernel(aff, words, s_out, deg_out, block, mid, arrived, far_words, mask_rows, far_mask,
+RELAYS = (
+    0x7accaf61ef321c32e1df2a1e3681db5c8d734d9070d8862ccf2c3786ada0dc1b72639b60db96436b581a964fa15e3585ef915c3af1215bda5595433850333404394832844513c030140d03c0208414,
+    0x7ecc2f8ca236c923dcbb2accb6ed73acde8e4c9d383d0e2d9bf03613456b20fc96785d1af99603635c54bda358d2d43d85494e32bcc33b4a51bcd308c4a1cc8d,
+    0x734bd2d4a5304b9254b11b4a1174990d4811c459074490c46b0545b064,
+    0x7b4e53e4f1374d53a4ad3447d0f4690b4eb3f1ff014,
+    0x73db76bda7735c8a5dbd69588a1d78a5568b7377562677137567c3763c9cd028717594d5b772132d4d2515b33153c54d333f0f32cc3709433,
+    0x1df7d9d779967f59ed6f96c395c76fdd8ae29f7558f5fdc56d5477f380bd3a73659d65cc16f37f1f5b1578ace052899c7cd7c4d5732747d0f51c1548524c7c170530f01504c1c,
+    0x1615a951525a0105af6404b4a5880c9801e02146970065680295804587409014a0,
+    0x1fa7bdf27a9f8369f0305e8349ca760a175db2625a2740c834da55c572700a31f50d4b8b02a0,
+    0x65e879fe779be5f95e4f91e3f8be279fb1f9065ed1b3ec7b,
+    0x1ffbdeefb9edfb3ec7afeb7abea7a7eeef9bdef1b238de86d9b36c5bed01b,
+    0x71aedb6addb36c5b83adb239db038dae1b8df6a86a365a6998de955a239858978e3e4594970e21784e56f983704e63d9813a5434f9159c5612b8c32f8d56c4e125883574861a0c139084154601f40300451,
+    0x1e6b7afdb96d5ad6a5a56f0616e85d6e07616977e8a5e65db41cf986c85364a701bfac1a7a7e55771805de359ce7922aac5487b5413b631321841d9442a571411313c53d284400a02f09004,
+    0x76eaba6e8ba0ebdeaf6b98eb6d6eb090ea8a3b708ee6ed822b82b5093b0b8e22ec0e,
+    0x1fb7cfb3a8e7bbe2aed4e96fc2e886ef9742c0ae913a14,
+    0x1e1f2fd9eefc9ea7a1eaf7ffb899e6f81f3879ed869d878bdbf95eb863e3851dd8931985c13039dec53180360d04b11729ce007cfd19cd11e0300800705c31,
+    0x1f9fc7e9feffff47efff8c1f98f3f3f91dc7be167a62ff55297d31146e32c41e17bc30c56380b3290b8118940c7c753403df0980796420c7f4972c100064dd1dc2715c5d,
+    0x767a1da761d2739f1821c47819e6718c62988619898,
+    0x6c7a9e4789fe4f11e771d4731e8689926419b8f895801b8ed4f22c93a1,
+    0x788aa228721081708c2f484110140301c,
+    0x7e8f226862138330e80d07c,
+    0x6f6ada768d9f6759965591675cb6dc3c26e730c0ae2a0a6280959a51f064c3664173,
+    0x756af336c5a966d936168f635bd0fd47652456fcf90127d323416c400d,
+    0x7f9be689224881a048,
+    0x4c8,
+    0x6547515e55134fd9668587e668d40681e,
+    0x1afa8e9fa6e3283a93b34,
+    0x786c9b56c1b36b1ad6a3686ada4d91ac1a8616799d69864159956804c9458a6a802a1ac26,
+    0x1f9bc6e9b46fdae6edaa6bda9699a56f8606f07a1e0761699b6d057649949f914cc86e141b80434f635b6021896,
+    0x1bdfcfe17bfa979fa5c970af2f,
+    0x1d173fb7eafa7e22fdd829dca277c37,
+    0x1ddef7ade97c1e57a9d2fa1df76debe91d9781d5771d178c27161e318450735dd125d9131cd84c5193c49121cd5274711483207411,
+    0x71ef9ff7f5fc7edf87e5f67cdf279dfd0b1e1799ff175e275dfd169fb13df9151cb7dc7511df31c44abbc45806ad1b56b1,
+    0x6e379263f878780e4640e6261124bd0e460b0c090d4,
+    0x1f0fa3f1783d1bc4d1343fd39449944213ecff2ec,
+    0x1dd655764942d435,
+    0x1e5495cb31c,
+    0x636dc372c435bbc3d52eb0244252b0b33e54df779425c89f240e2574fd1403d08855,
+    0x1ecbf0f4392f8ba2e0bd3fd742ed75390b5c,
+    0x69581585415d51a432,
+    0x1cd6d59d6356d5ed5b52915849,
+    0x15eabea7a1e5f95e37bc62f83e,
+    0x1f79da8437ed5afeb7a5e6f87e,
+    0x1cbb0eb3a8e9ba4e83a456ba2c4812e7146e5583a,
+    0x1fbbebf3baee3b6ed3be5abbf6bf90ee9f432fae3,
+    0x7afa7e4f8bdaf62c6bd9f27,
+    0x1fbeafe7f3fb7e3fc98ef66d5f2bc5f1bc1f,
+    0x1eff9fd7f3fc7edf9f2bf8fddf67fd557f19850df,
+    0x112ffff7f7fbfdff5fc8f3fc1e,
+    0x70cbb2ccab26c8b20c7b1ac5b14caf3a1430c88b6e289fa37b5cd534ac4b74319b033b6e31186a2342d,
+    0x7ace33e5db34cfbfe2f9fcdeb7e3e8b6de0b2dc0b0db3767dbac3a36e7632839b63c936238354a635ae328cd60c9e30cb4,
+    0x618761fc2613c2705c,
+    0x1fe3dcd731c9f25c8718cf084debcfc,
+    0x67d9763d7f5dd6f713676d35f693576534f6136f1d36cd1d6b5733f5535b4fc4cd1334cbc260b32649314c9d0cc4d,
+    0x7f9fcfbdf4fd9df7b3c77bce4fc9e7389dcf79d4f5cccedcbceb39cdfb8cdfc875f36710d3cc7c1cc5d04c45,
+    0x15b5bd5f4fdf543d,
+    0x5a592255,
+    0x1aaa4a7a9aa5a92a3a836,
+    0x7aaf3bdee2b6ad2aca7288a,
+    0x1f779dd770dc76edab64d9f62a9763d5a9fd6748d4f4ac,
+    0x7daff78dd9fbddf6eacf6fdaf659834c952a9d437e5877de328ec4744bd7fc1,
+    0x1c6ebb96e1b76dbb4edcb46cfb2bd1711c8b,
+    0x7bbdefcb9ed8b42cbb03c7b,
+    0x1b2f6cdf34cb32aca324c6622c6e5796b3605b0b94300c276dff4ae08fc27,
+    0x1bafcceb38c8af2c85b0cbb26c831ec9edbb4acbd1740a,
+    0x7c1e070cd06ccc06c1986217860c707f4685ccf53d3e933b5b161e4f74c6f334877cbcce1d127362f5428633431f3912bc3add39ed935cdfb4cdff81dc53cc614fda451cff24ce700da23942c2880400594,
+    0x1fb3cceb38cfaf6cfefabcb2ac9b3f37b36beefb35b75bc4d8cb4edb7adafa4e53a96133339ccfe676cebf96d53cd23f91f4271ea244dbf34d672b1072fd0919efca50bc138472cc0e1e402,
+    0x6f4a72d4772b4572944b2548d21475194551a461114310d40905401018,
+    0x1ed394dd354cd2c4c53dc992742e174,
+    0x1de759eeb2df2aedeaaaddaa8d8b72abab1cb2adca2a5e9f20a579db8f382d8b22ce9ca6f217b899c65e8257262594df4dd45588a5371220941e10ad90f013,
+    0x799ea7ede376dfab0de2a6d836ddd29adc2adea718d976aa92a5c774ad873c27f0de773a227b026157c6dec21fa424720278905508853887c15c050dc1c,
+    0x1b56b59d6558d5857d7c0217a0657605d720015995e6c0566804d6401660078180,
+    0x1fd7d5f1745b1795d5665cd70089605c56a0796b998279a2639882ed31619702158a5605a54040109364c012439,
+    0x6ceaba8e9ba4e8ba0e7b9da63adf56a7f87ddf2b95f47c7f1d81f,
+    0x1f3b6ecbb9ac3b7abbbbfffbe6b6b9fd7fc68ebb4bfc1aa7f73e183f,
+    0x7c6e8f46d8fd6c1bb6c8ec6b8f76d5a86cc711a8ef1baa26e850598eb1b5a7188de6c067a78e3a846de68e816996695abe6c61e58e1648d466f9814c4e34855e6d901398a32c4c10b8633d8482447e21823144210b41601801,
+    0x786d9b26b9b96a9a46c5bd1e46f6dabe1d4606f04e5296d1ada4ae06968c71ebfac1619f19067e8d991499de704e839c6b43d113c4de558af4589e318a11c4410f8461d831,
+    0x6efabe4f73d0fc7efb23e5f5efa7f5d7f03c9f,
+    0x1dbe2f53fdbdfca722caf6ecb90ec5f,
+    0x7c7f5fa7edf67b9f77f3f57bdf6fcbed7bbe47abe779be2493e077920fbfdf77bd875118f5dd2449e1f66e30740cf7757f640a431c8f674f954047478a03c014180b51bc550805f0640f,
+    0x7fbf9ff7e1f97c9fdbeeec7a1f5b89f3bfbe17e3e8f69fff6df7f73e9fb416741157a427045e107c23e6c0443ee3c2dd3e4c0df254802c09013c150fc000c011,
+    0x748ba288c1e28e5e8789eb7a5fe15ad27f0586f8d4641ba131866f0feed8743c8f41,
+    0x7e4f1384d9387c9e0db9f77a9f589ae67c870391f01b0e66b8626b0681a0de6698ea984e69048688c060aa01,
+    0x6b9a66596e5594e4d92e4990e534,
+    0x1fe7d9e675937339c6579070f902879,
+    0x7d669756a59e99da567d9b65d9364595465d5735cb7b40778c1d305db03c0d0,
+    0x185ac9bda49ad99685ff445cb63dc9715c6a,
+    0x1e25d5d2709b66a99a515865f94248a,
+    0x7e9ea7b9ca779516f9b2679,
+    0x14a91334c561186e,
+    0x7eacccd6c4ef325876b4eb3a4d269cc36,
+    0x726d1b06b1a8699af6e0606a59e6959a6d8721b85666da8190526bc59670506d0ea321e63745c36c49e1a9565446109bef1dd433c421,
+    0x1f8786edb96e87e6feaa6ec567c07dadc62bc0dabe93567116b485e34450361a0928d763ac83,
+    0x1a0a62909c780967789477098231d6229d4248847408e22880712c62,
+    0x1e8b62f1f4281f2269f0241ee219e37b0aa2889a2a8160,
+    0x1ffb97c5ef791f4b89ed795de785e0061dd7701275dd6041d2b380d64ed1729c804d4561941a,
+    0x1b1fabf8287f03a099ed6e036081e37d03de85b2069df775b00b80c755cf6a8047c57321dad5a4416,
+    0x74571545913f451125cd105490c52146511405,
+    0x1f17a581da43944b7b561af0c10941c,
+    0x7a4e1364c90481d07c,
+    0x1f913244bc4a9264393544d0a4ff3dca3024,
+    0x718dd735bd71ca56fc9d635855f57c1b5655553d4b56c1301d4230d490,
+    0x7d8fcbf5f57b5e5755c56b5f4175e7135357782575bcc310bc055ac015,
+    0x6457957971545d4085,
+    0x685894e96963561515,
+    0x13790a22946,
+    0x1bf89e,
+    0x1e0741c86e1a8601785c1e8de0c8d815b6e34844d384a1f1401d96c6,
+    0x7a1d8701987e3d8e4168421e994700044,
+    0x75f97dff6bd7f2fc7f,
+    0x1fffbfe7f7ff5ccf19d97,
+    0x610ce8f07f99e2f0b2249b43d09f,
+    0x710ac290941f06c27e5c1504f0fc6c5de2c4712f85e,
+    0x1eb32cc32ecb33bca326cd722ca720c9721c7319cc8d8cc0e8353183471233b1a93707c6188c38c5c30d582e0c20b01c,
+    0x74ce72acdf2a5932dcaddec9f1ac8f16c7712c5f0fcf8fc3430bce8e2662ccc71b83760c61302bd0c6868828,
+    0x1cfaec3331ec52be0b03c,
+    0x1ffb9cf7838,
+    0x1f771ed37bdcb71da76cd9f63dab61d777129b6f2aca728ca0d5f5f25353d6c9724c8982b51d3c86d2c8520b432,
+    0x7edf378df436dff7b0c36fdbb658f49fdecb92a3694dc9bdd4a18cca2d676925e118374258483c74856275921241938112,
+    0x1c3fcdabfb5d16959552453cef38a54,
+    0x1f3f8fd3dcffd775d108d755a43902f214d52b879,
+    0x77ac6ada9ea1a6e93a3284a,
+    0x1febdaeeb9a3f82e76bf35688a0a83d0e826,
+    0x1d773dbf66aa77e49758c5256c431fd4e88c,
+    0x7aef3beafb7fdfb38ceab84d33ddaa70cfeaccef6e4a339d8337d6a5cac0ec3,
+    0x1e276bbaeab7ae298ed2b22c77d3ecf,
+    0x78b61c76,
+    0x7bcdf33c37efcb731b8f32c772ac932487f9ac5309c4b17a94a702776c7c19026972680d02c8c014080,
+    0x1ff33bf73cc9f26c8b37e47098ec06c1f0daaffb20e69fe4b70,
+)
+
+
+def unpack(number, bits):
+    values = []
+    while number > 1:
+        values.append(number & ((1 << bits) - 1))
+        number >>= bits
+    return values
+
+
+def kernel(aff, words, s_out, deg_out, table, block, mid, arrived, far_words, mask_rows, far_mask,
            col_sums, row_sums, row_shares, col_shares, near, far,
            load_sem, word_sem, leg_send, leg_recv, hop_send, final_sem,
            row_send, row_recv, col_send, col_recv, pair_sem, out_sem):
@@ -49,12 +304,8 @@
     def group(n):
         return pl.ds(pl.multiple_of(n * TILE, TILE), TILE)
 
-    def place(cx, cy):
-        return (cy * 4 + low * 2 + core) * SIDE + high * 4 + cx
-
-    def steps(n):
-        shift = 2 * (n % 16)
-        return (X_STEPS >> shift) & 3, (Y_STEPS >> shift) & 3
+    def place(cx, cy, cc):
+        return (cy * 4 + low * 2 + cc) * SIDE + high * 4 + cx
 
     def mirror(device):
         return (device % SIDE) * SIDE + device // SIDE
@@ -78,22 +329,40 @@
 
     to_partner(words, far_words, word_sem)
 
+    kind = (((high % 2) * 4 + (y + 4 - high) % 4) * 4 + x) * 4 + low * 2 + core
+    for outer in range(16):
+        @pl.when(kind // 8 == outer)
+        def _():
+            for inner in range(8):
+                @pl.when(kind % 8 == inner)
+                def _():
+                    sends = unpack(SENDS[outer * 8 + inner], 17)
+                    relays = unpack(RELAYS[outer * 8 + inner], 10)
+                    for n, value in enumerate(sends):
+                        table[n] = value
+                    table[CHUNKS] = len(relays)
+                    for n, value in enumerate(relays):
+                        table[CHUNKS + 1 + n] = value
+
+    relayed = table[CHUNKS]
+
     def leg(n, carry):
-        dx, dy = steps(n)
-        relay = place((x + dx) % 4, (y + dy) % 4)
-        direct = (n % 16 == 0) | (relay == partner)
-
-        @pl.when(direct)
+        entry = table[n]
+        relay = place(entry & 3, (y + ((entry >> 2) & 3)) % 4, (entry >> 4) & 1)
+        slot = (entry >> 5) & 127
+        number = entry >> 12
+
+        @pl.when(slot == DIRECT)
         def _():
             pltpu.make_async_remote_copy(
-                aff.at[rows(n)], arrived.at[rows(n)], leg_send.at[n], final_sem.at[n // 4],
+                aff.at[rows(number)], arrived.at[rows(number)], leg_send.at[n], final_sem.at[number // 4],
                 device_id=partner, device_id_type=LOGICAL,
             ).start()
 
-        @pl.when(jnp.logical_not(direct))
+        @pl.when(slot != DIRECT)
         def _():
             pltpu.make_async_remote_copy(
-                aff.at[rows(n)], mid.at[rows(n)], leg_send.at[n], leg_recv.at[n],
+                aff.at[rows(number)], mid.at[rows(slot)], leg_send.at[n], leg_recv.at[slot],
                 device_id=relay, device_id_type=LOGICAL,
             ).start()
 
@@ -104,26 +373,21 @@
         def _():
             lax.fori_loop(first, last, leg, 0)
 
-    def hop_of(n):
-        dx, dy = steps(n)
-        source = place((x + 4 - dx) % 4, (y + 4 - dy) % 4)
-        target = mirror(source)
-        return target, (n % 16 != 0) & (source != target) & (target != me)
-
     def hop(n, carry):
-        target, used = hop_of(n)
-
-        @pl.when(used)
-        def _():
+        @pl.when(n < relayed)
+        def _():
+            entry = table[CHUNKS + 1 + n]
+            source = place(entry & 3, (y + ((entry >> 2) & 3)) % 4, (entry >> 4) & 1)
+            number = entry >> 5
             wait(mid.at[rows(n)], leg_recv.at[n])
             pltpu.make_async_remote_copy(
-                mid.at[rows(n)], arrived.at[rows(n)], hop_send.at[n], final_sem.at[n // 4],
-                device_id=target, device_id_type=LOGICAL,
+                mid.at[rows(n)], arrived.at[rows(number)], hop_send.at[n], final_sem.at[number // 4],
+                device_id=mirror(source), device_id_type=LOGICAL,
             ).start()
 
         return carry
 
-    legs(0, FIRST)
+    legs(0, CHUNKS)
 
     def start_load(n, carry):
         load(n).start()
@@ -176,8 +440,7 @@
         return carry
 
     lax.fori_loop(0, SIDE - 1, share, 0)
-    legs(FIRST, CHUNKS)
-    lax.fori_loop(0, BEFORE_SUMS, hop, 0)
+    lax.fori_loop(0, MAX_RELAYED, hop, 0)
 
     def share_in(n, carry):
         other = (col + 1 + n) % SIDE
@@ -194,7 +457,6 @@
     near[0] = row_total
     near[1] = col_total
     to_partner(near, far, pair_sem)
-    lax.fori_loop(BEFORE_SUMS, CHUNKS, hop, 0)
 
     wait(far_words, word_sem.at[1])
     for t in range(groups):
@@ -230,15 +492,13 @@
         wait(far, pair_sem.at[0])
 
     def hopped(n, carry):
-        _, used = hop_of(n)
-
-        @pl.when(used)
+        @pl.when(n < relayed)
         def _():
             wait(mid.at[rows(n)], hop_send.at[n])
 
         return carry
 
-    lax.fori_loop(0, CHUNKS, hopped, 0)
+    lax.fori_loop(0, MAX_RELAYED, hopped, 0)
 
     def share_out(n, carry):
         wait(row_shares.at[col], row_send.at[n])
@@ -269,8 +529,9 @@
         in_specs=[pl.BlockSpec(memory_space=pltpu.HBM), pl.BlockSpec(memory_space=pltpu.VMEM)],
         out_specs=(pl.BlockSpec(memory_space=pl.ANY), pl.BlockSpec(memory_space=pltpu.VMEM)),
         scratch_shapes=[
+            pltpu.SMEM((CHUNKS + 1 + MAX_RELAYED,), jnp.int32),
             pltpu.VMEM((size, size), jnp.float32),
-            pltpu.VMEM((size, size), jnp.float32),
+            pltpu.VMEM((MAX_RELAYED * size // CHUNKS, size), jnp.float32),
             pltpu.VMEM((size, size), jnp.float32),
             pltpu.VMEM(words.shape, jnp.int32),
             pltpu.VMEM((groups, size), jnp.float32),
@@ -281,10 +542,10 @@
             pltpu.VMEM((2, 1, size), jnp.float32),
             pltpu.VMEM((2, 1, size), jnp.float32),
             dma((groups,)), dma((2,)),
-            dma((CHUNKS,)), dma((CHUNKS,)), dma((CHUNKS,)), dma((groups,)),
+            dma((CHUNKS,)), dma((MAX_RELAYED,)), dma((MAX_RELAYED,)), dma((groups,)),
             dma((SIDE - 1,)), dma((SIDE,)), dma((SIDE - 1,)), dma((SIDE,)), dma((2,)), dma((groups,)),
         ],
-        compiler_params=pltpu.CompilerParams(has_side_effects=True, vmem_limit_bytes=24 << 20),
+        compiler_params=pltpu.CompilerParams(has_side_effects=True, vmem_limit_bytes=47 << 20),
         name="exchange",
     )(affinity, words)
     total = size * SIDE

time: 166 us -> 137 us (0.83)
  the two profiles are of different devices: /device:TPU:185 before, /device:TPU:1 now
where the time goes in v5:
time: 137 us; the launch traced here: 136 us
  Pallas kernels  131 us (96%)
  other arithmetic  3.02 us (2%)
    pallas_call x1, Pallas kernels, on_device(): pl.pallas_call(kernel, out_shape=(jax.ShapeDtypeStruct((size, size), jnp....  131 us

profile of v5, /device:TPU:1, one launch (start us, length us, event | category | flops | bytes accessed | tf_op | source)
XLA Modules:
  0.0 135.7 jit_solution(14985346087722026002)
XLA Ops:
  0.6 0.0 copy-start
  0.6 0.7 copy-done
  1.4 131.3 %exchange.1 = (f32[1024,1024]{1,0:T(8,128)S(1)}, f32[2,1024]{1,0:T(2,128)S(1)}) custom-call(f32[1024,1024]{1,0:T(8,128)} %aff.1, s32[5,1024]{1,0:T(8,128)S(1)} %bitcast.4), custom_call_target="tpu_custom_call" | custom-call | tf_op jit(solution)/shard_map/exchange/pallas_call | solution.py:523
  132.7 0.6 slice_multiply_fusion
  133.3 2.4 %multiply_multiply_fusion = f32[1024,1024]{1,0:T(8,128)} fusion(f32[1024,1024]{1,0:T(8,128)S(1)} %get-tuple-element.4, f32[1024]{0:T(1024)S(1)} %bitcast.5, f32[1024]{0:T(1024)S(1)} %bitcast.6), kind=kLoop, calls=%fused_computation | loop fusion | flops 2097152 | bytes 8396800 | tf_op jit(solution)/shard_map/mul | solution.py:553
Async XLA Ops:
  0.6 0.8 copy-start

commit v6 on v2

--- a/solution.py
+++ b/solution.py
@@ -10,25 +10,280 @@
 TILE = 128
 SIDE = 16
 CHUNKS = 32
-FIRST = 8
-BEFORE_SUMS = 12
 LOGICAL = pl.DeviceIdType.LOGICAL
-OFFSETS = (
-    (0, 0), (1, 0), (0, 1), (3, 0), (0, 3), (1, 1), (3, 3), (1, 3),
-    (3, 1), (2, 0), (0, 2), (2, 1), (1, 2), (2, 3), (3, 2), (2, 2),
+DIRECT = 127
+MAX_RELAYED = 69
+SENDS = (
+    0x1fff07bf83bfc1cfe0dff06bf833fc18fe0bff05bf82bfc14fe09ff04bf823fc10fe07ff03bf81bfc0cfe05ff02bf813fc08fe03ff01bf80bfc04fe01ff00bf803fc00fe0,
+    0x1fff0200f3dfc1dfe0e7f0180737fc1afe0cff063f82ffc15fe0a7f0589d67fc12fe08ff043f81ffc0e6316ff033f817fc0afe04ff01ff80bfc04fe01ff00bf803fc00fe0,
+    0x1d979aff80a12942a1f9a8cc987c62240c4b13980013a5231221e128c078542acf1a1d0f8b070e43a6e161c8a8b44070122914340799c30441243062b8188428ea0226001,
+    0x15151dcd4c61c94313fff07bf810487dfe0e7f04494f7fc1afe0cff063f82dfc0401430f1b86cebfc0c1339ff04bf821fc0ffe06ff01434d7fc09fe000221ff8020c62fe0,
+    0x1f7f077f837fc1a760cff061d02ffc16720e0cdd5b80203b46a09ff049883e93915c087f03ff80a16ae5206ff031180002ab3c057f024d011fc0726037f0107007fc02060,
+    0x1fff07bf83bfc1cfe0dff06bf833fc18fe0bff05bf82bfc14fe09ff04bf823fc10fe07ff03bf81bfc0cfe05ff02bf813fc08fe03ff01bf80bfc04fe01ff00bf803fc00fe0,
+    0x1402ce198bece57622f31954a1980fb2266eae913f838b256502da894d18b49a50402ca293ce8a8824d34289d90c0a44032b26271892460944241fe0386b18388a1640002,
+    0x1783477f82a05793d2e7f06bf831fc17fe091415bf81840532b2f056d3f80a187023230527c1423fc0a15277f024448814e70f26ff06c0f42006bfe00013a3f8040443fe0,
+    0x1a06b613074b227fe0f8c9dc78eca2351a3984b41104bfc0e4011ff04460fc226d123900b30e87a1e6a0a30ff02cd85e82240ece059a0b0720e6206c3168a408f60e80000,
+    0x158857ff8104d3efe0509377f839fc1bfe02017583db5fc19fe0c7f0383eaffc140b6aff04ff825fc11fe038d0c3f80410cffe06ff033f813fc06fe0000317f807fc01fe0,
+    0x1fff07bf83bfc1cfe0dff06bf833fc18fe0bff05bf82bfc14fe09ff04bf823fc10fe07ff03bf81bfc0cfe05ff02bf813fc08fe03ff01bf80bfc04fe01ff00bf803fc00fe0,
+    0x1fff07bf83bfc1cfe0dff06bf831fc17fe0b7f0652dc20154fe09ff04bf821fc0ffe077f037f819fc0bfe057f027f811fc07fe037f017f809fc03fe017f04457ea70e0fe0,
+    0x15ff07441fc879650037f0281af89a14480da484910348611400b9d8408332538e2c0a91e34a01e4e091e0f86c080bd83a081a0988b9412ce2a0314020786001c20e000e0,
+    0x1d9f098241009ff157b1a0f9246e5d3c3f19940e4dc624838137e863d4ac7414f40f778c0c8845c242b1d15080b036d21c230103850c015ca0c240d16ff0082c420420031,
+    0x1f7f02501fbfc1c742d7f065c8b657d86e2f8ed5da0abfc146029ff0584ba5fc1158287f03d50862f6e4e26ff0310897fc0a3c247f00403cffc062e22ff0109085fc00122,
+    0x1fff07bf83bfc1cfe0dff06bf833fc18fe0bff05bf82bfc14fe09ff04bf823fc10fe07ff03bf81bfc0cfe05ff02bf813fc08fe03ff01bf80bfc04fe01ff00bf803fc00fe0,
+    0x1f82a2ca21e7f9efe0eff06ff835fc19fe0c7f05ff82dfc1c064aff053f827fc12fe08ff043f81dfc0dfe0198e33f80e028016c57f027f811fc06fe02ff013f805fc01fe0,
+    0x1dff067f831fc1647c69245ff82bfc13fe08ff043f81ffc142dc5046309f78048efe020a49c07f41c2bfe09040a3f80dfc05fe04810fc1c47fc02fe00ff0740c41fc1e015,
+    0x1816f13f803fc110c6f07970ab1a4bd308258bf649b1227d722cf8ee1c43ba33941ccd039182bb62b9216cc08e3c4b2c028e10c283f303b2a0b2a0ac405e0c230003c200c,
+    0x168e5e05e3e618c47f90546cccf85d9d117d16607f81c1115034b9462d07ec4983019a106786f1e3d9917c50d64c4f0e29910fc303420ffca19890dc8171902704098001c,
+    0x1f99ce0fb32739538ce16cc8db2c67902ecda1ec7f828538d22cd1ceac831c438ffe0b99ea7f8265faa16d60fe1c33502f8412c286e0ff83c13e20cc308e80133a020100d,
+    0x15922fd974a10b8fe0a7f04bf81dfc0dfe057f07987729dbd3b9b256a3f82a91bb55d8a16e9374dfc174bd7996f0a647fc133dd6136c0c75239a71fd2054883f4200a005d,
+    0x1984ae8889c0eb82025abf34d37e5e551e20ff030c37c524a2cde93918fbb8464928dc97ed058b63e5214218ad1c836c43af0e280ce94636e264412d407e882b62064002d,
+    0x170c5fcace4586c19a68b5d847604c7e2737911c42f563c7d2130836a8df901d7c1f348b1ec74ce59da1b330a1e454c8207811328e75c3cc411d50b31841d014c00073013,
+    0x150ac4832a21a62fe06859c02ab8234e08a287c740003fc0b06ad07d1c1bb2175f1c1b04d241281fc1e1a1a03d2002a60b44048601d6c604c0677161180d5450700a0f121,
+    0x1f7f077f837fc1f156d7f07045a61cd8fe0aff04bf82218d0fe068533ff81610d90d667f027f811fc170b637f0581d9c28a5fe050330bf80e08d405620130c058200c0fe0,
+    0x1b11d443a9ffc06fe0829f6c81989fda1e6f8db0ff8163b4832e17f064719227581a6080ddc61bc32d5166285d5051ba2ed2126e0ab0053a626cd0e6707b28218e1ac4046,
+    0x1fbf764c6baf5dc0b6d3c779cf840c7b71ebbb761bf8208766de3ff01405aae1d46be9b670005e2d5d269e83273d979ab9ce61e5ab731579295ca47e41b718cf8835c31de,
+    0x1f8dbf449fc2efcfe0dff06bf833fc17fe0b7f0342aebfc14fe0805de039e7fc11fe0584dbbf8100b720c767f03c21ce16e400b283babf813fc06fe017f007f80606e0fe0,
+    0x1b083f855f4317813730c2d445ee2d6e179d977c83de01429097a0a58c15e225600172862f456de217c13b6875e446d80c330fb4065ac36ce117f0910826901ed4002203b,
+    0x1d94dd4c2fed3fd62fb92de97bc806f95aff33fd95bc20b5454f98ddc933f8bff04afc2dfbc92e2afed42f728fad03d89bea36f4a1fa0a3ce53e51af303d8c3bc407e002f,
+    0x1a1d7d92ffa38ef3dfe0d3c82ef430ff157c8b3ac26f028fe13730b79047ee24e309f6ff06c3de620e7fe08873d435e018ee0b76053881fc009e1fe05043a425ca00e8057,
+    0x1f27a33f83e4398424e26a59012ebf143e4e8fe48f12ab7113a4da5a40e111fc0f3643ff017f807fc0e344d23a2cc905fc0d5e80ff028b901fc092c49a0a1861320784104,
+    0x188b73c0efa683f171b9326cbe2029de375a980e0351c58bc2f59160d04c9621da2355077647d504021fe048d2b08e4820ad13528509c3d6619a2075183083f80c09d603e,
+    0x1f8bf3028bc46e308ce8fbf0b1cc12c206cd0ebeca1f232f8267494d5889ee2ee5006504a5081ce3f521e7a89bc469e622e40ca807bbc51dc1aed107082d2c31d1fc000a7,
+    0x1b8c46c5513fc14134f153880f389d7f61bca45f566f0897a4fba9c5c8450c089649b2012403d26696e0d4898584165e596d39b5935a8aec6008821b0016302d0e1165014,
+    0x1f9fa3c917a7686fe017f064b2f86a8a1c5c19a40892e5e80fe0b16a38711012ad1a4a13a1009742fec16498fa6c4be43a8914488ca5423d622870a4285a0c093c0601004,
+    0x1a242e7f82dfc1e4159a32d7f82288b2fe08212a3f81e80bf17d71e2f0fd5a70a5fe027f00ff8186cba5f917f061765660b75795142ec9d5240a0fe0386298354200bd13d,
+    0x1d16b44ca7e73391c6f1bcdc61ba6736166e15ccc51b64f345eac11cc16a800a891c97afd38216a3b2d52a90bc8c52481b2a48a5a5d08225836c830a388b14118c3341049,
+    0x1f91343f83a40c519b7832f8bd8810e3057e0f3080df434db29650228016cc19f92764012dc0fc200b8256a88337f82818d621688534c7d9c10d21765833303d9204c7076,
+    0x1f0a8eff83a223010cf86b6048384a8c0aea8ae343b22278b0cc508e3828101f860ac909a1423341e39221b7f0101b29fc0302cb848cc70440b09121004e1c385e0621041,
+    0x1d9b6fc6c7469a4074c196e4af6c61b729d9976d4976059b123d7156b4875851be191e190ac7f544da81dd9067744c4e49a619d2906bff8283c2315d4880883f4209a005d,
+    0x16ff033f83e87c9fe0f20f1ff80dfc1b3aee9ff64e3b47bd734ec1df58c3aa6fd42ce1ff04493a65bc2fe0915f71f2a05f4f18e710f2c4b9437c0fe0408f141b880bc100e,
+    0x1cc0557f83a6ddc77aa7f03bf81bfc09fe0d1977ce7ae5dd835eb1574ccf91fc1231e88e76dd69e35d025e37f030779621de0d650570ff805fc070be0800942781fc0401e,
+    0x19ff059e22ac303fe0f928408b34538c20cc93e3419f04b810cba11e247b3c46081cce8f85c7838361230488ee186b1c378518c58ce3c680e2f8a160000b905b362a0214c,
+    0x1c077f8346245bd15ab115cc5eea0dee13b90b5f04e9e195911a8085fc27c809f40fa58f4dc1ff4342d09a6045281e92117b05140250407ce054605a1805080e8a096001a,
+    0x1c0293bf83e93fa4af5ff05d1bfc8bf442fe81a27f83883e6fe0d9ffccf3f277f036fa9bfbccbe463e5fe0894fb4abc7fc02fe0b01907f801fc0a20f612fa06bce2fe40ef,
+    0x1da97dc0db2a1fe277c2779bf82899e3fe09a47fd1fea5cfd2179227f10fdc7dfa3df61d7d8e7d669f135f5187bcbfe004ed2df414787f80e49e923f20c79467c1fc0213f,
+    0x1f0ce44532ffc15fe0d89e53f821fc0e10cfb2a283b1ffc1c7a4eb1a1c2334ba8cfe0584e65b1080f89fe0c2ba23f80dfc0104cb2aa49510bfc03fe09a5a0bf81a8280fe0,
+    0x1e382756530251f11ca98297f836cc944559172c4ed74ac9e0fc8112b8d55e40ad295ca622c955028a9155b86630360e10a31355024102e2c94820953006041d664880015,
+    0x1b09aec620c0334168a83a90127e0e922e7f1dbbc190bfc03029d1bbcc523266fd123b96bb889c3fc0c207e07c2461c1fc0a024806c2c4a222ee2009685c20420e0b18043,
+    0x1f7f0281e0e397dfe0202673f835fc19fe0c7f05ff82dfc15fe0a7f07c0d27fc12fe08ff043f81c09effe06ff06c1fd9fc0209b5ff027f811fc06fe02ff00ff803fc00fe0,
+    0x1588cf1a129fc1b644f90e698127fc11fe0ca9a61692ea29d2a0b27a55393c2f8efe0922a41091e6e8afe0106cb4c9184a88fe048da1c610c2285fe0201a000907fc01fe0,
+    0x1f146b3f832b0bb6f54ff069b56cacbf0bda2a2a3f81a3d386b59292dd9d7a2da6fe08a82d56d608cb353507f03d3d5c78bc07d51c29d1d4a54a41b558848c654405a1175,
+    0x1eff03c226023bcfe0d7f067f831fc17fe0b7f057f829fc1210e9ff038235233460ca8ff02c917e23cdfe0613b17f80e36ca06ed8da8ff83c0242fe00ff0201b41fc04069,
+    0x1f056647df80decfe08846741f17fc0e1574095e0574e24e60b728165c4f542cc90d6d06490170608c2017a05483f802019f3b5b172ecb56615b50fd8072c8375e09ad0bd,
+    0x1803d64d9f83b96347286b3d613e8a14327b81f48c1fc7a112a7d9b84c7330621d0afd0fbb899ea3aeb24750dba481cc2ae81c760b81c51da17840e7186b8419c40ae0007,
+    0x19156e827980d5f2d6892378ada044dd2967903086e5c3cdc27668e304169634db2560015648d9430d821648b35c7d9028d61d63893546d8c20d419620734c5d8614c50b6,
+    0x1f8387bf81c6ac61e6eff073f837fc1afe0cff00412b1fc17fe0b7f057f829fc13fe097f047f821fc0ffe06ff033f817fc0afe04ff023f80ffc05fe027f00ff805fc00fe0,
+    0x1f7f0696db9fc1bfe09a6367f81e88d8fe0aff053f823fc17496e831fc27a1fc0007b61c3590d9dfc123f65ff0080f5205c8fe03ff034e59454c5fe027f00ff80c44c1fe0,
+    0x1f9c86c6321fc1a1e091ea27f832560f3a489aa38c12e421d02f615a2ca92636142873ff0604814468102b40ca58300a2695080185a13f81a120210430287003fc42e00a4,
+    0x1b9f0b1a56a743f3d199a0f8e462643d3517970f0c45a543b2b15930e89454443921148f0e0745030361b138b0d0644c24321512870c04448102e0b118308814420820031,
+    0x1e7f06ff835fc18fe0b7f053f825fc19607e83f43f81ffc175c777f037f83ec6ecfe05ff05549ca1b6afe04ff04d19fcaae302a081b44f9d1fc063273ff013f80046e2fe0,
+    0x192c3fd95e0a0fbfe0d7f07975f3fc18fe0bff05bf82bfc14fe09ff047f81ffc0efe067f0754dd7fc0afe069e3a7f811fc1c4573ff01bf80bfc04fe000838ff805fc01fe0,
+    0x1fff07bf83bfc1cfe0dff06bf833fc18fe0bff05bf82bfc14fe09ff04bf823fc10fe07ff03bf81bfc0cfe05ff02bf813fc08fe03ff01bf80bfc04fe01ff00bf803fc00fe0,
+    0x1fff077f839fc1bfe0cff078a66dfc15fe0a7f04ff825fc11fe087f03ff81dfc0dfe067f02ff815fc1739d4ff0687e51fc07fe037f017f809fc03fe017f0604643fc00fe0,
+    0x1a0cf7c987a6e3e221d198ec806c5a391a1c0aedc58664e3c0ce508ed430501ba516388f8c8205e362310320998812182e2608d5878c0105216210833848b808400e6d001,
+    0x181a1e4dcf40d9ffe0f7f077f81a5c75333e7f04cb4d4487bfe0c7f03ca4effc0e27348f1ac84ce28681739026dbf829fc060f38ff0100759fc000941ff0142cc5fc01033,
+    0x1fff07a103bfc1c820dff069f833fc187a0bff059e029fc1376097f045d02a778f72081da39b0022bad6a067f02d9015fc0958047f01d400dfc0548027f00cf805fc001a0,
+    0x1fff07bf83bfc1cfe0dff06bf833fc18fe0bff05bf82bfc14fe09ff04bf823fc10fe07ff03bf81bfc0cfe05ff02bf813fc08fe03ff01bf80bfc04fe01ff00bf803fc00fe0,
+    0x1e7f06bf833fc1b622faa957f83ca258502ea294918ac765710da1b934c89c5653fe08ff024a09617a722287f01468881a4ffe01049042099fc0afe047f00ff80c1320002,
+    0x1cb51717caed05b5d2b2f1695c9c1d3e1bd8ac1612c9e94534125864c0e492704d312f8b6a894ba29a001347f0505f6a1da71f2905698648a384c09d20b10c2c841441012,
+    0x1d1381c12a42f8402af188f0c84203db2e1a8f860b05e2396261e948ac3b324a34201b8e8b428263631181304e0c01a02e2504070a8b048541e3f08400182428501622061,
+    0x1fff07bf83bfc1cfe0dff0083775fc19fe0c7f05ff82dfc15fe0a7f00c07e7fc12fe08ff043f81ffc0efe06ff033f817fc0afe04ff023f80ffc06fe02ff013f803fc00fe0,
+    0x1fff07bf83bfc1cfe0dff06bf833fc18fe0bff05bf82bfc14fe09ff04bf823fc10fe07ff03bf81bfc0cfe05ff02bf813fc08fe03ff01bf80bfc04fe01ff00bf803fc00fe0,
+    0x1fa03f7f839fc1afe0cff063f82ffc16fe0aff053f827fc12fe0d895c7f80828d0fe07ff03bf81bfc0cfe05ff078a5d5fc09fe047f01ff80dfc05fe01ff00bf803fc00fe0,
+    0x1fff07bf83bfc1cfe0dff06bf833fc18fe0bff05bf8280be01c0aff04ff825fc11fe087f03ff81dfc0dfe067f02ff8061b0afe04ff023f80ffc06fe02ff013f805fc01fe0,
+    0x117f074148605f233cf3107c3e76bc01fe0cad0717c2ea41a5d00000e1642a8c165308a20513c206c134b071903d0c18600d3f0594028dc124c082f0391018940824050d0,
+    0x1f7f07618b9fc1b7e2d7f065e8b1fc17742aff051b8ac275366297f04570a1fc0f52277f0353099fc0b42257f024d091fc072c237f0149089fc031e217f0045081fc1f066,
+    0x1fff07bf83bfc1cfe0dff06bf833fc18fe0bff05bf82bfc14fe09ff04bf823fc10fe07ff03bf81bfc0cfe05ff02bf813fc08fe03ff01bf80bfc04fe01ff00bf803fc00fe0,
+    0x1fff07bf82e067dfe0182c73f837fc1a4eccff0550b31fc102ecb7f03483140274fe09ff04bf823fc0ffe077f033f817fc0000c4ff023f80ffc06fe0080c17f809fc02fe0,
+    0x1b8e2bc3e15fc14279b092cc765c111f0d1f336303e881127fe0eae60ff83699891992834204e6418350748840f037b479993bc8022e057160422fe0300083f81a0581014,
+    0x1c09e2c333e7271223f1b9c15bea1b8408ce999bc80f8566e4afa01a3468f64e7228bd109b060d5fc093cf984e0413323a6832fb8a99c48cc5fe522fb0798003043fe3083,
+    0x1c9463c45cc14ff1bcb926445eec418dfe0a0e60c0e26319809480b62435dc2987fe06096786716219d17c507648150225fc15c20026c4710159a0bc2836541f04058001c,
+    0x1205cabf81847b914b3ff02c7b6a838914dc1587c782e460e1a8409ef8602c3a0d16cd04a9443682e100cb186ef440261e0608c885807f824169c060780808234013bb000,
+    0x1fff07bf83bfc1cfe0dff06bf833fc18fe0bff05bf82bfc14fe09ff0001665fc11fe087f03ff81dfc0dfe067f02ff815fc09fe047f01ff80dfc05fe027f00ff805fc01fe0,
+    0x1ea3ea983b88bbe422b86b6cf0929bd93823a4f58d8b087b334270bd30a36a77b12e2a1aec0b0a45fa20c6f9693480b43e4408a58a9187b5e57a014d403d0c308a2ba1002,
+    0x1b1311bf83065bf4bdb9869057ea5dbd49d9966d00ce255be29280e1710758305b3dd1867c84494245a39d7926e4c75a39a909210278427d631a007b4056b84f4e0445039,
+    0x1f109cca8fe2fc502a205d0c02ba27d2283083d4498f83e70223d01f3c80f6366e1c307f03460f2326b143c0a9a840ee22690e3b059a028ea1267083a0399818d80a62003,
+    0x1cff07c66b1fc17fe0aff0785ea9fc13fe0e0853bf8361d4dfe05ff07456b4194afe0b0551ff82410d113a784517f8180d5011a402524368c0cc2fe007f010058605c105a,
+    0x1f95d7a23bae3c8fe0e37f6e13b4dbd982ec35f506aae4f5678eab3f4dcba4cbd164e829f3d5b980b4e44e2ff02cfb9a6bca2ee494f1c838c27c40ce1ff007f80407c004e,
+    0x1f4077c8ebaf9dc69edbb75855f4e1d863e7873dd6faab5d44fe5863cd0f942d7905391e71c36c3fc0c09781b744bf8815650377157246f9a05480fe30970c178005c2017,
+    0x1c948604aec4a1710b998e3019ea42120eb894e03f8102b0d1ec790e7c33e8320a14c58de183b0e2f8e0ab106c7828360f6906b188e1012c2179d08f803870100a06fa020,
+    0x19986abf80ffc1b132715693f82818fa1128853c89f6010f90f240412c67522dbe0f730317435de11780d26023dc248a04f6072f837f01dda0c2205d0ff0540c8600e003d,
+    0x1f2eff5dbc7fc1c72fdacfe9c3f0a7f76cfb28fe4908c47d51e2a27fcd6bfe3a521a28a4fbd3bd883ee16280992d03da1e41fe0381920dbc1fc0a042498f9483c402440ef,
+    0x1eba7f16ff6ddfa55fcb57dff830cdf5fe0a7f04bf82cc9f0fe09af7b7f822b1eafe0f1d5bd1fdc8dec3ff4ff07c86d67de835f20039cafcdfc03fe017f0146fc3fc00fe0,
+    0x12ff079393e8f9d4c4e22e6929307a97484da1e59193283954241ff04cf9286e923a4898a40d91e5a80fe0695a38c9184e8b2c450fa24890e3a881e4309a1051041681024,
+    0x178d090957c889c1b1da0274e50e2dbf07db1e268d52870932f489a248a51c60902546050b48d14102b2144932186d10388211528c264344624980b108625c14400095011,
+    0x1e10b4450b63eda347b8eb58c9e82ad52e7909b2c313e3eed0e6807b4ca9cc4f4e267e8dba829bc43c70a4784b3081f22fc210ac0cba479c0064806627f01401862ae1004,
+    0x177f06c8cf07df92139800a8161a09961f3ea03d474f878f41b3d1c3a40e2e6cf11939183a3f82058fe1d737f03c5cd848e1fe02081ac4cc004870f318e3884dca019f01c,
+    0x1fa7af1096ec73b4058ff043f83c9ab83a5389c33f83a96b5345d21aabf83282a8fe068484c996c6aae1e5a17abc934dfc0b185911a90414bfc030a517f00409520600fe0,
+    0x1fa22dff83c7cb4fe0d1e2b7f811fc010362ff0101ef070a2fe0a9b283f82464bd6798172f1965e54b33d5db148c1632c1313755902b8b55434ac2153072a46d6c0927095,
+    0x1a11ce471adfc0cfe0483e8c0bfe365b262f0c96890ba52d8222788cd480b82e531e2209ac870ae2a501a2506cb460a2224b162705920488e0f260e2101c9428821240042,
+    0x140d5dc2fc828eb0b370a6d01ff830d62996894fc9598213525948379c1cd41d32219d0b340767028c30539893786da220dd1160015ec358a11b90b6103498165e08c1019,
+    0x1302f795a683f9c529fabcb85b13fc0202e98de2c53202b9a4e9eaace52a5a2797489da6ca84b308f36449aa0c9c3b247b240cc406e44f246138f3a9084b3092400b85fe0,
+    0x1d960e89eb2bd3725a48b558868e155f5f9aa32d06eba5dbc1fdc2a4cc776459a30be8956c05f4409cf13d7136f9155a45aa11a6106ac47503da009a30e684078a31a40bd,
+    0x18ff0695399fc1852ee96b5d4395fc154eef9ef23f80dfc196ca27f04d33bcc3524aedacd0ff80a0ab046e17f03d0381fc0e3aea23d2cc3b86fc92aeb17f1c8b9a1bc108e,
+    0x1c24764bff61c8d170a22707f81e44f21ff99f730542aa9501bf8a7578151c65cb13f28679c47cc0c7f35e2021f4c7ae108309f1027f0051251da1be4077281fac088001f,
+    0x1f9fe3493f87b962ace8efe9c22e06ec1efd9ce246bea6f8616fc8bf84087ccb1126c998e144bf0af0f24c409fd001c61feb388724c0833c8176004f916e1caa204f8a1ac,
+    0x1e9463cde64217c0fb69b4e437d2157f69860d6ecd71429ab0fdd2a41c276c951e5583086e1460a1da405da9165d16284188fe0996444ce0615a203d81243826c009a103b,
+    0x1f1df7c61721e5336fb1fc83f83673d234fe1ffbcb3f07bed28fd0caac9be86bfd102818fdc49501eb10c5612f2473c62b55082712f9c5bd42fe50ef083a9819441be4025,
+    0x1fff073f8227cf90f7d9e7dc25c615c9fe0c1d7f55eec71e7fe02ff07907e461e4fe08177e936c5fc15057715787f81a49e0fe09a95d0b7d43def23f61d5ac67d021e625b,
+    0x1f3aa686b09fc17804f89e59f107fc15328eb9a50c2100622fe0e38a44ba36de8f2c8cb6a41b930d68d6849b3a298124c68c12c730a03f816b68740431ea24330a3281064,
+    0x1e8a67d2455fc1e471c8561ff836ac9a338b9a270b52c8cb80f427f051256a84b33f591f2c4d55e68b033517f038b55a50a50146112ac855238a811530728c1d4204a0015,
+    0x1dff078333e379d0accff02c30f8339a08cbff024692dfc1806caff04ff828278604397f047f81ffc0efe0808e37f80e1b8cfe0283e2bf811fc03fe0100f1000c20380fe0,
+    0x1a1325c3f20449e11398d1ac2f1c11fcfe050f26ff806059afe0cff063f82dfc111d7aff04bf819fc09fe03ff017f81005e4fe07891fc3d1a2061fe0304183f804047d013,
+    0x1fb0ae5716a43365a5f2ead16178b6b2505d2cae0731e37314c5e8ce34a2762f8c18c5a6a285b26a6a710cb88e183b121f8508c827a901b1c86a304c41da880b020b8000c,
+    0x1f156c0667851bf27d47f07497744daf159b926ec8f6845b85159906e487643db61dd68c6d515582dae39558a6c4675421a917d387698574a19a413d1836881f4201a003d,
+    0x1a06ec82b59fc1e06e985ef05a7e2339129885d2bf80ffc1810937f017f83a1f350c91ff0402345fc0d06dd05ca4136c32af0a9b81cec0b9c0fa1066581ea00a41fc0402d,
+    0x1c074c4176a2d1f0d917f0280768291d0999894785e1e211c158707403f82060f905958646c4e1a4cfa1184054583e240d290d830441c2e080d0505860248c0e020517019,
+    0x1408c1810120619286f7f05c99860336246e7f05489be5ad3206a0ad28039dfc121e6104a447199fc101a6003a2ff83a56c5fe0081c3c61b652cd0aad11b1c51b03ac4066,
+    0x1c180e52d6a583f3f19940dc65a2483e3b17110f4cc6080bc31168e0ecac5470ba29160b0a0bd5628361f1389090ad4c18221f52830d05c4608320f10062bc1c420029011,
+    0x1903f1c00400f03009fff06003bdfc02186eff073f837fc1afe0cff05ff82dfc15fe0a7f04ff823fc10fe07ff03bf81bfc0cfe05ff02bf813fc08fe037f013f803fc0510a,
+    0x1b24364fdb7fc183d678c1ebf82680d123740c3a465e074df33abff053f81dfc15336618348b59bfc1e0b35871f0ae8dfc02fe051331c758a0c641161873740cc00161076,
+    0x1aff04869fa2b8d3a467f068b83e36f92a0823a60a03c32f118707f05c902c5f09167705fbc8038320a1c8202f9451e82eeb160989ba0400e1ae2047182b9828360e0102b,
+    0x1b09364e53424fe1f6a0835cd5201cd32b46863448d1c309f15750437445d034bc09f4894b075241cfb1563882603d9e04f50b62862181d8800eb01f182304058000c2017,
+    0x1410b7da1e04f5332bea5bf989dc475b60728bb6571f8777754758cd5141c3fc124c7d22bc521ea86ef427482f34e1d872ea14bc0191ca9cc0b441c7b0090c29c41ae0007,
+    0x1fff07bf82a88fdfe0e7f060f5f7fc143b75963ebf833fc17fe0b7f04ff825fc11fe087f03ff81dfc0dfe04943b3f80a15661171033abf811fc010573ff013f807fc00fe0,
 )
-
-
-def packed(values):
-    word = sum(v << (2 * n) for n, v in enumerate(values))
-    return word - (1 << 32) if word >= 1 << 31 else word
-
-
-X_STEPS = packed([o[0] for o in OFFSETS])
-Y_STEPS = packed([o[1] for o in OFFSETS])
-
-
-def kernel(aff, words, s_out, deg_out, block, mid, arrived, far_words, mask_rows, far_mask,
+RELAYS = (
+    0x1e32cbd0701b079ca872ca078ddf36d9074d6a221c35eed724c706c3ab73cb72836064383623c15617bea5915216b5cf815c35bda33867c6956548c8140ced010632144f00c4503d541040503402,
+    0x7eceb2abba34caa3bcc32cccb6edb37839b363b524dd0dac7924fb8f257b62fb1464de29463e8578d8d53dc5615834b50f414e32bccd20ca51bcd308c4a23473,
+    0x7f4e5354e12f4c92d4b92947d284552f8910f4791c4610b4510647b05453044,
+    0x7e4f53a4cd3649d3048d13441094fb3f1ff014,
+    0x73db769d9763dcd702b56b5876028d5c2dcddd6095d58ad37d6bc971022f67365633871fc5ed353c9f35151c74d534cce53ccfc2cc370cc25,
+    0x1df75dc759fbf7f5743d5d6719af742be7759f6c27f755bd7d33f69cd95e2e4e758f345ccddcb9615994c2acdbc6517c662533d5732747d0f53c1f0c51549314c5c0f01504c1c,
+    0x5a58a585b7545a01259816d880e580129780a570069215a0874e0114490d429014c0,
+    0x1ff7e9f27e0ea7c0c977de27a0da780c26c5d02a9db60592720b32d5414898d700ab038b82a0,
+    0x63e879fe779be5f95e4f91e3f8de279fb1f99b3991b3ec7b,
+    0x7fef7bbee7b7ecfb1ebfadeafa9e9fbbbe6f3ba6cae2f9bb56cdb16c1b,
+    0x73afdb8aedb56bdb83c8eb6c0e768dae3c0616b8683a25b6826235d9e36a6c170e7e4d949985fe60e01315437859e459a14190930cf557a515848337991338b5259215740600ce430488310551807d14401,
+    0x1e6b7af5b76c5ad6a5a56f85f6f05d67a7a1d7b815959681b6161b415a6fe55b21b7a8197b31885be555ce359c182a049c528635a4845413a0763b4c959151491313c53d28440290280bc04,
+    0x1cbacea3a4eddf298ba8f7396eb6d2eb890ea8a2296cee68a1b2382b5093b0b8bb4880e,
+    0x7cfd3aae53be29ecce76fc2e886ee0bc5c884e7e0f4,
+    0x1e9f2fd1eefc9e5fb1e87abe1fe624781f389bf1869d678bdbfa5eb851e7833e38931f8541075e1107318c3418029d2c35d203f41f19cb1080f80c01701c31,
+    0x7e7f1ffffbff8e1fdfc1fb889fcfefdc7d6187b5ed86539f49d74451f7f31b8d32f0cb290d82ec560e7b023003d18cf640740b98b1dd64097400b03747715c1911c5d,
+    0x181d8749d0731ca721c47c620669966318a62195819ba2,
+    0x747c9f07a1fe4e922771d6739ea6899464199826006dbb02c93a1,
+    0x768a22685a1081f08c374641101c0500c,
+    0x1e22086a0ac560e81509c,
+    0x1ddb56c5ad69da1675996558f68dcb66e7e2f0b62b8aa278979d427484e5064c364c153,
+    0x1cdaf6b72b68d9b65d916168d6fd476ed569158492b7f3fc016ec00d,
+    0x759a65e9224881a048,
+    0x4c8,
+    0x18d21457974552566185e668d40681e,
+    0x1b7a8ea7a6e8283ab524e,
+    0x1d9b26edae6d5ac6bda86b5aad93626d0701a86367d9e6a064159976784c955a602982a1ac26,
+    0x1f9bc6e9b46c1bf6a9b169da56f866691bc1e8616e05c6d859651929f914cb8506f00ed3d8b6d008688496,
+    0x1d97afc5fbfd7ea5adc970af0f,
+    0x1d17ffc7e6fa7e2268bf7bde1f30837,
+    0x1ddf37c5e97d1e77b9e57a1d2f75e6765ebe81d7779d578425169d17844f77c5475c4f841c974c4d14649121cd5274711483207411,
+    0x1cfbe7fdfc7e5f87d9f57c9ed7a9e37dc2477ddb7fc627f45874dfb1e4771d44b739f3115f11bc4abac45806a91bd671,
+    0x1b8e6678f6750e24c09c4512f4708e4e3024e70d4,
+    0x7e3f0fe5e8f86e0fc4f1763d93f4f53eb69964213ecf04ec,
+    0x1f56357e4942d435,
+    0x1ed495af2cc,
+    0x7b0e4ab0bee5095bd54697dc8910a4a62d4cdfed5de48932388bf2c0bd1c0221543d,
+    0x1fcbd2fc3c2ecba2d0bd3fd6e2e577378bdc,
+    0x19d5c5415f51a432,
+    0x715bd605ad6556d66d7350915849,
+    0x57a9fa3e6f97e578fe2783e,
+    0x7fea439e76b3ebfb56b7a9eb987e,
+    0x76ed3b2ec3aeeaba8e93a456ba2c6014e5148e4d83a,
+    0x7ebfbbceebb8e9bbe5738eee7bf6e9f03b0cbe,
+    0x1ebedfc3e4fe99ef52cabe9f87,
+    0x1fbf89f3fdfc7ebf97d9b3bd3f2bc7f1bc1f,
+    0x7bfe7f5fcff1fbfe7f8fe1f67d5fe55d4ae4bf,
+    0x11affff7fbcdfebf77d3fdd11f23c1e,
+    0x1c32cca324c8b20c7b1cc5b24f5312ce8568bf1b883607d0dcd6b4cc6352dc0c8c21ac33b6a31188a1b42d,
+    0x1f338cdb3e5d33e2f1e6cfb7c2eb7e3d8b8dc3702bb6cdc8f27a378ea9ee39b64d98e2d6094a9396d2ab1c2b5a3278c3450d4,
+    0x1961d8360dc2707c,
+    0x1c637ca725c871dc6714cf880debcbc,
+    0x69d9f63d875fdbcdddacdbd676738cd7d7cddc6cd5d5cded54d3d4cd4d4f1133cc9834c9c2ccfd264931cc332343d,
+    0x7dde77f3ee7d3f73b3fa793e7389dcf99df753d7333cf313b4e9376e536f2133f0dd74d0d1705304c25,
+    0x1f55cd7f55d4743d,
+    0x1616a8dd478,
+    0x64a829ca5a92a2590a,
+    0x78ad2beecaacaa2a6a6286a,
+    0x1ff7bde772dd76edb366db1ebd8aa9d8f5dd5f4ad4f4ac,
+    0x73af774dd9f7dcf71db2add9f56a63599974694a8ed677de2a8cc3f42bbffc1,
+    0x75bbee9b8edfb6ed1b6acfb6bd1711c8b,
+    0x7bbe6f3b9ed7b82d6b26d0b16c0f,
+    0x6abaff8cf736cc31ebb328c931b88b1d96e5ece81ac4656c0309decb0087c27,
+    0x76bf7eebf33bfeb34c9af2cbb236ab26c831cc96d7b32c7d1742a,
+    0x7c1e06ecd06ccc06c1986217874b831c1685acf5161f4d4cdcfb4ccd21df35bbcce1d1374b6ca1ace33a90ec187546bd6b84efc74d938127b3ad734ce1b3cda469c03005df6954724cff31cbf688c50b0a26d004,
+    0x7cceb38cdb32cc33fb9b3cb931cce4f535b313c2fdbb4f1ba4d6d9cdcb83efb7cea56cccccd33f54eff8ee6744f9c9fe27d08d38fde7a899f59cac39f143a467c70b309c4e03879008bc,
+    0x734a72f4872d4572944b274851d46517455164450842d02415004,
+    0x1fd3d4ed394c1374ff2a4d5264ad1584e014,
+    0x1de739ceb2db368df2b1ae2a4dd2a2dcaaeab72caaf21e9722a7a95e6edfce0a77d8b0275dbcb098a672825953c47e224dd25608a53701e4884510ad90f013,
+    0x1ee799ba7edfebcde374dfabaa9b71d8376acfa9cc2abd736aa9f24a435dd7ee3c873c2479dc27ba295f226157c17ae298977809c24151c50865408051f05705c1c,
+    0x1c56f5ad6758d585f81f5f0360315b5c8175b80056e599566a04564016600701a0,
+    0x1fd7b5e9785c1795b2f75a9755e8285d0335916c0796d9982b9a265988219782cd600a5755e958149480e03a4d912439,
+    0x72ebbaceaba6e93a2e839ee4e8eeb7e9f87dbf3e95f2387f1d81f,
+    0x7eeebb6ed6afad3adaf7f0ea6afef9b7fe995ac7f94afc1a37fb3d183f,
+    0x7c6e8f66c9bd6d8fb6c8ec6ddae399b56a0f2acc6f198e26d8545b4623ada3179aba78f018e9a37c6de905c658e7e59a5687931859236859e518e375921578a3384e618cb12844e24423358481f886144210b40605801,
+    0x7a6e1b46c1b96a9a46c5bcae4771bdb6ad47e181bc1a5925c44e5a2ba19da71cfb1eb0611a05a6af9b18da5e705263215131d0f3c4fe4d8d12bc6b3189e458811c4410f87611831,
+    0x193e2f4bcafd7e5b97fe74efa7fdc4f7fc9f,
+    0x1fbfcfa3fff9bfbfe6cef22ddb2646f0ec5f,
+    0x1e9fb7e1f47ddee7cdfefc5ed7f3f6f9df2f99e37812ef9ee8f79e4f7122f75ebf7bd675dd2466daf41e104121d6c17f3bd3f6f550290a74c08f4651e280f00d06021c751bc2017c550640f,
+    0x7c7e5f67eef57c1ec7a1f5bebe277df4fabd8765f1fa7d8fcc117ac127312703ddf0740db8f9701123c2dd3e44095200df3404f2c0350003f0c011,
+    0x1aa2888a1e8b1fb789de7ade97f854b51fc17196651ba139886f0feee0783d0f61,
+    0x1f9384d9324f9f8783767a9f77d6267b2e47c072381ec3b86a3a1ac199a83a06066990a985068846680c060a9e1,
+    0x1ae6999e5f976579464d9265b40e4b4,
+    0x1f6799de759b65393e41c028b91e7f4,
+    0x1eda568d9a9759e56d996458d665cb63d1574ecd72de501de306cc175c0d0,
+    0x6a9e5a767a619859f97d9765dff0258f7fd09715c6a,
+    0x1e25d5ca709c66a97a4b5965994246a,
+    0x7e9ea7f9d27b949739ba6f9,
+    0x16a91334c561186e,
+    0x68adcf53ccf131daf3b4cc6acc36,
+    0x746c1ae6a9a6691b1681a96f05e69db6171b21b0661759668860149936b4723399a1a8e1190d9170c9e544aa458611dc26fbd433c421,
+    0x7e6f1f67e1bf6febb6b1be1e6bd182d8772fc4d07e3d596bc916180e5168da68a531558cb38c43,
+    0x198a42889a7809e261dc249da231d6229d4248847408e2308070ac42,
+    0x7c2e0ba7d8b22c9f0241ee219f37b0aa2a0982b8140,
+    0x7fec5377c5ed799e479ae5785de775da759db7881e055d276818039d4b3811729cb62ec604d4561941a,
+    0x7d7e1f07e2fe0f0287e8207cda97e03ded81c77df4095b208597751ee05d8f6b0047bd476a5732a4416,
+    0x705d1185517b4610e531524cd0a52146511405,
+    0x7a5d97a7f92e54946b935a1af0254843c,
+    0x7c4e9344c10481d09c,
+    0x1f93846c992a1204bd0e45d31c2925ca3024,
+    0x772f5795d56f5a5675956fc7c1b565575b71553d4b5641501d61c08c35,
+    0x7d8fd7b5dd735d62d5e42354d4d525718fef30c434d156f0056b0,
+    0x176579916056952521670,
+    0x685994c97163559555,
+    0x65e378ea22946,
+    0x49e,
+    0x1d8741c06a198641805a158620407a33044d286a3f1401d9706,
+    0x1f87c1e06e1b2e21c8eed704219192700044,
+    0x69f8fe1f63d9f2fc7f,
+    0x1f7fbf71f97e7c872bd77,
+    0x1de8907f97e371d4348924509f,
+    0x1dc330b42b0a42307c2de5c1fc3c13c5c59e3c4712f85e,
+    0x1f33acd32ecb33dcab37c9b2dc9329c8323c731dcd0d6cc8f034f2e34b1e34311c724bc58c8c1f1035983c30dd82e0c20b01c,
+    0x70ca97bca335c95e2c9f1ec6b25c6321c6f17c530ec373839190b331e67e04b130c6d8c6848828,
+    0x1df96c3b2fed52de0702c,
+    0x7de1e39e,
+    0x1afbfde376df775dc371daf6ad97712876b27f6729b6327497d735b25756d649723c88d374d21b4982c8720b432,
+    0x1fb7cdeb7f0f43ded372dfca7df4af48f6cdecb92a35dddcb52a609c9359db4a784f538a48254605c94856224fd7c81940132,
+    0x7effd7b5bbee5ad62f954c433e5423ce2,
+    0x1f574fa57042354443d04595950bcae2e494,
+    0x79adeb5ab69fa6691a2a86a,
+    0x7faf6bba8ea1a6613a2282e0a83a0f426,
+    0x72da2b9dd771d9f63d6b38453089431fd6e8ac,
+    0x7aefabadbabfdfeb8cdb2ecf76847268c933bd8337dcf5ec4258ac0ec3,
+    0x729c2eeb92e0972dfb4ac8b1de8f,
+    0x1dae87bbc76,
+    0x7bc8ff9cf6f5cbf34cb325cab21c9b2487319c7f98c4b07c9c1f25689d7c1b05c960268d02c8c014080,
+    0x7fbfb3dceb30c8e06c173d0cfcfaf4aff066bfecbb0,
+)
+
+
+def unpack(number, bits):
+    values = []
+    while number > 1:
+        values.append(number & ((1 << bits) - 1))
+        number >>= bits
+    return values
+
+
+def kernel(aff, words, s_out, deg_out, table, block, mid, arrived, far_words, mask_rows, far_mask,
            col_sums, row_sums, row_shares, col_shares, near, far,
            load_sem, word_sem, leg_send, leg_recv, hop_send, final_sem,
            row_send, row_recv, col_send, col_recv, pair_sem, out_sem):
@@ -49,12 +304,8 @@
     def group(n):
         return pl.ds(pl.multiple_of(n * TILE, TILE), TILE)
 
-    def place(cx, cy):
-        return (cy * 4 + low * 2 + core) * SIDE + high * 4 + cx
-
-    def steps(n):
-        shift = 2 * (n % 16)
-        return (X_STEPS >> shift) & 3, (Y_STEPS >> shift) & 3
+    def place(cx, cy, cc):
+        return (cy * 4 + low * 2 + cc) * SIDE + high * 4 + cx
 
     def mirror(device):
         return (device % SIDE) * SIDE + device // SIDE
@@ -78,22 +329,40 @@
 
     to_partner(words, far_words, word_sem)
 
+    kind = (((high % 2) * 4 + (y + 4 - high) % 4) * 4 + x) * 4 + low * 2 + core
+    for outer in range(16):
+        @pl.when(kind // 8 == outer)
+        def _():
+            for inner in range(8):
+                @pl.when(kind % 8 == inner)
+                def _():
+                    sends = unpack(SENDS[outer * 8 + inner], 17)
+                    relays = unpack(RELAYS[outer * 8 + inner], 10)
+                    for n, value in enumerate(sends):
+                        table[n] = value
+                    table[CHUNKS] = len(relays)
+                    for n, value in enumerate(relays):
+                        table[CHUNKS + 1 + n] = value
+
+    relayed = table[CHUNKS]
+
     def leg(n, carry):
-        dx, dy = steps(n)
-        relay = place((x + dx) % 4, (y + dy) % 4)
-        direct = (n % 16 == 0) | (relay == partner)
-
-        @pl.when(direct)
+        entry = table[n]
+        relay = place(entry & 3, (y + ((entry >> 2) & 3)) % 4, (entry >> 4) & 1)
+        slot = (entry >> 5) & 127
+        number = entry >> 12
+
+        @pl.when(slot == DIRECT)
         def _():
             pltpu.make_async_remote_copy(
-                aff.at[rows(n)], arrived.at[rows(n)], leg_send.at[n], final_sem.at[n // 4],
+                aff.at[rows(number)], arrived.at[rows(number)], leg_send.at[n], final_sem.at[number // 4],
                 device_id=partner, device_id_type=LOGICAL,
             ).start()
 
-        @pl.when(jnp.logical_not(direct))
+        @pl.when(slot != DIRECT)
         def _():
             pltpu.make_async_remote_copy(
-                aff.at[rows(n)], mid.at[rows(n)], leg_send.at[n], leg_recv.at[n],
+                aff.at[rows(number)], mid.at[rows(slot)], leg_send.at[n], leg_recv.at[slot],
                 device_id=relay, device_id_type=LOGICAL,
             ).start()
 
@@ -104,26 +373,21 @@
         def _():
             lax.fori_loop(first, last, leg, 0)
 
-    def hop_of(n):
-        dx, dy = steps(n)
-        source = place((x + 4 - dx) % 4, (y + 4 - dy) % 4)
-        target = mirror(source)
-        return target, (n % 16 != 0) & (source != target) & (target != me)
-
     def hop(n, carry):
-        target, used = hop_of(n)
-
-        @pl.when(used)
-        def _():
+        @pl.when(n < relayed)
+        def _():
+            entry = table[CHUNKS + 1 + n]
+            source = place(entry & 3, (y + ((entry >> 2) & 3)) % 4, (entry >> 4) & 1)
+            number = entry >> 5
             wait(mid.at[rows(n)], leg_recv.at[n])
             pltpu.make_async_remote_copy(
-                mid.at[rows(n)], arrived.at[rows(n)], hop_send.at[n], final_sem.at[n // 4],
-                device_id=target, device_id_type=LOGICAL,
+                mid.at[rows(n)], arrived.at[rows(number)], hop_send.at[n], final_sem.at[number // 4],
+                device_id=mirror(source), device_id_type=LOGICAL,
             ).start()
 
         return carry
 
-    legs(0, FIRST)
+    legs(0, CHUNKS)
 
     def start_load(n, carry):
         load(n).start()
@@ -176,8 +440,7 @@
         return carry
 
     lax.fori_loop(0, SIDE - 1, share, 0)
-    legs(FIRST, CHUNKS)
-    lax.fori_loop(0, BEFORE_SUMS, hop, 0)
+    lax.fori_loop(0, MAX_RELAYED, hop, 0)
 
     def share_in(n, carry):
         other = (col + 1 + n) % SIDE
@@ -194,7 +457,6 @@
     near[0] = row_total
     near[1] = col_total
     to_partner(near, far, pair_sem)
-    lax.fori_loop(BEFORE_SUMS, CHUNKS, hop, 0)
 
     wait(far_words, word_sem.at[1])
     for t in range(groups):
@@ -230,15 +492,13 @@
         wait(far, pair_sem.at[0])
 
     def hopped(n, carry):
-        _, used = hop_of(n)
-
-        @pl.when(used)
+        @pl.when(n < relayed)
         def _():
             wait(mid.at[rows(n)], hop_send.at[n])
 
         return carry
 
-    lax.fori_loop(0, CHUNKS, hopped, 0)
+    lax.fori_loop(0, MAX_RELAYED, hopped, 0)
 
     def share_out(n, carry):
         wait(row_shares.at[col], row_send.at[n])
@@ -269,8 +529,9 @@
         in_specs=[pl.BlockSpec(memory_space=pltpu.HBM), pl.BlockSpec(memory_space=pltpu.VMEM)],
         out_specs=(pl.BlockSpec(memory_space=pl.ANY), pl.BlockSpec(memory_space=pltpu.VMEM)),
         scratch_shapes=[
+            pltpu.SMEM((CHUNKS + 1 + MAX_RELAYED,), jnp.int32),
             pltpu.VMEM((size, size), jnp.float32),
-            pltpu.VMEM((size, size), jnp.float32),
+            pltpu.VMEM((MAX_RELAYED * size // CHUNKS, size), jnp.float32),
             pltpu.VMEM((size, size), jnp.float32),
             pltpu.VMEM(words.shape, jnp.int32),
             pltpu.VMEM((groups, size), jnp.float32),
@@ -281,10 +542,10 @@
             pltpu.VMEM((2, 1, size), jnp.float32),
             pltpu.VMEM((2, 1, size), jnp.float32),
             dma((groups,)), dma((2,)),
-            dma((CHUNKS,)), dma((CHUNKS,)), dma((CHUNKS,)), dma((groups,)),
+            dma((CHUNKS,)), dma((MAX_RELAYED,)), dma((MAX_RELAYED,)), dma((groups,)),
             dma((SIDE - 1,)), dma((SIDE,)), dma((SIDE - 1,)), dma((SIDE,)), dma((2,)), dma((groups,)),
         ],
-        compiler_params=pltpu.CompilerParams(has_side_effects=True, vmem_limit_bytes=24 << 20),
+        compiler_params=pltpu.CompilerParams(has_side_effects=True, vmem_limit_bytes=47 << 20),
         name="exchange",
     )(affinity, words)
     total = size * SIDE

time: 166 us -> 137 us (0.83)
  the two profiles are of different devices: /device:TPU:185 before, /device:TPU:57 now
where the time goes in v6:
time: 137 us
  Pallas kernels  132 us (96%)
  other arithmetic  3.02 us (2%)
    pallas_call x1, Pallas kernels, on_device(): pl.pallas_call(kernel, out_shape=(jax.ShapeDtypeStruct((size, size), jnp....  132 us

profile of v6, /device:TPU:57, one launch (start us, length us, event | category | flops | bytes accessed | tf_op | source)
XLA Modules:
  0.0 136.5 jit_solution(14894636618759799080)
XLA Ops:
  0.6 0.0 copy-start
  0.6 0.7 copy-done
  1.4 132.1 %exchange.1 = (f32[1024,1024]{1,0:T(8,128)S(1)}, f32[2,1024]{1,0:T(2,128)S(1)}) custom-call(f32[1024,1024]{1,0:T(8,128)} %aff.1, s32[5,1024]{1,0:T(8,128)S(1)} %bitcast.4), custom_call_target="tpu_custom_call" | custom-call | tf_op jit(solution)/shard_map/exchange/pallas_call | solution.py:523
  133.5 0.6 slice_multiply_fusion
  134.1 2.4 %multiply_multiply_fusion = f32[1024,1024]{1,0:T(8,128)} fusion(f32[1024,1024]{1,0:T(8,128)S(1)} %get-tuple-element.4, f32[1024]{0:T(1024)S(1)} %bitcast.5, f32[1024]{0:T(1024)S(1)} %bitcast.6), kind=kLoop, calls=%fused_computation | loop fusion | flops 2097152 | bytes 8396800 | tf_op jit(solution)/shard_map/mul | solution.py:553
Async XLA Ops:
  0.6 0.8 copy-start
